TPU v7x, 32 devices: a whole 2x2x4 slice. The times are simulated.
32 devices in a mesh: cfg: 2 (over y), req: 4 (over x, core), seq: 4 (over z).
Axes of the slice: x: 2, y: 2, z: 4, core: 2. Of those that a mesh axis runs over, the one named last changes fastest.
Arguments:
- image_hidden: bfloat16 [2, 4, 512, 1536], P('cfg', 'req', 'seq'), may hold values from -6 to 6
- text_hidden: bfloat16 [2, 4, 160, 1536], P('cfg', 'req', 'seq'), may hold values from -6 to 6
- modulation: float32 [2, 4, 10, 1536], P('cfg', 'req'), may hold values from -3 to 3
- attn_weight: bfloat16 [1536, 5120], P(None, 'seq'), may hold values from -8 to 8
- proj_weight: bfloat16 [1024, 1536], replicated, may hold values from -0.1875 to 0.1875
- mlp_in_weight: bfloat16 [1536, 6144], P(None, 'seq'), may hold values from -0.15625 to 0.15625
- mlp_out_weight: bfloat16 [6144, 1536], P('seq'), may hold values from -0.078125 to 0.078125
- final_weight: bfloat16 [64, 1536], replicated, may hold values from -0.15625 to 0.15625
- latents: float32 [4, 64, 512], P('req', 'cfg', 'seq'), may hold values from -6 to 6
- guidance: float32 [4], P('req'), may hold values from 3 to 7
- text_lengths: int32 [2, 4], P('cfg', 'req'), may hold values from 1 to 154, 385 in all within a row
- step_index: int32 [4], P('req'), may hold values from 0 to 27
- step_count: int32 [4], P('req'), may hold values from 1 to 3
Outputs:
- velocity: float32 [4, 64, 512], P('req', 'cfg', 'seq')
- new_latents: float32 [4, 64, 512], P('req', 'cfg', 'seq')
All inputs are finite; a program needn't handle non-finite values. No bound on the sum of `text_lengths` on one device may be relied on, other than what follows from the above.
Results may differ from a plain program's by a relative error of at most 0.017.
Values may be sent and summed in bfloat16 or wider, within the bound.
A program may use at most 128 MiB of HBM per device.

v0:
```python
import jax
import jax.numpy as jnp
from jax import lax
from jax.sharding import PartitionSpec as P

HEADS = 16
HEAD = 64
STEPS = 28


EPS_NORM = 1e-06


def partner(value, axis, distance):
    mask = 2**distance
    pairs = [(source, source ^ mask) for source in range(lax.axis_size(axis))]
    return lax.ppermute(value, axis, pairs)


def modulate(rows_in, scale_row, shift_row):
    values = rows_in.astype(jnp.float32)
    center = jnp.mean(values, axis=-1, keepdims=True)
    spread = jnp.mean(jnp.square(values - center), axis=-1, keepdims=True)
    return (
        (values - center) * lax.rsqrt(spread + EPS_NORM) * (1.0 + scale_row) + shift_row
    ).astype(jnp.bfloat16)


def sigma_of(index):
    remain = 1.0 - index.astype(jnp.float32) / STEPS
    return 3.0 * remain / (1.0 + 2.0 * remain)


def split_columns(weight_piece):
    width_in = weight_piece.shape[0]
    head_count = weight_piece.shape[1] // (5 * HEAD)
    shaped = weight_piece.reshape(width_in, head_count, 5, HEAD)
    image_cols = shaped[:, :, 0:3, :].reshape(width_in, head_count * 3 * HEAD)
    text_cols = shaped[:, :, 3:5, :].reshape(width_in, head_count * 2 * HEAD)
    return (image_cols, text_cols)


def local(
    image_hidden,
    text_hidden,
    modulation,
    attn_weight,
    proj_weight,
    mlp_in_weight,
    mlp_out_weight,
    final_weight,
    latents,
    guidance,
    text_lengths,
    step_index,
    step_count,
):
    seq_size = lax.axis_size("seq")
    local_heads = HEADS // seq_size
    image_rows = image_hidden[0, 0]
    text_rows = text_hidden[0, 0]
    mod_rows = modulation[0, 0]
    local_rows = image_rows.shape[0]
    image_total = local_rows * seq_size
    text_total = text_rows.shape[0] * seq_size
    image_norm = modulate(image_rows, mod_rows[1], mod_rows[0])
    text_norm = modulate(text_rows, mod_rows[4], mod_rows[3])
    image_cols, text_cols = split_columns(lax.all_gather(attn_weight, "seq", axis=1, tiled=True))
    image_part = jnp.dot(image_norm, image_cols, preferred_element_type=jnp.float32).astype(
        jnp.bfloat16
    )
    text_part = jnp.dot(text_norm, text_cols, preferred_element_type=jnp.float32).astype(
        jnp.bfloat16
    )
    image_qkv = image_part
    text_kv = text_part
    image_qkv, text_kv = (
        lax.all_to_all(image_qkv, "seq", split_axis=1, concat_axis=0, tiled=True),
        lax.all_to_all(text_kv, "seq", split_axis=1, concat_axis=0, tiled=True),
    )
    image_qkv = image_qkv.reshape(image_total, local_heads, 3, HEAD)
    text_kv = text_kv.reshape(text_total, local_heads, 2, HEAD)
    keys_all = jnp.concatenate([image_qkv[:, :, 1], text_kv[:, :, 0]], axis=0)
    values_all = jnp.concatenate([image_qkv[:, :, 2], text_kv[:, :, 1]], axis=0)
    slots = jnp.arange(text_total, dtype=jnp.int32)
    valid = jnp.concatenate([jnp.ones((image_total,), dtype=bool), slots < text_lengths[0, 0]])
    block_rows = local_rows
    while block_rows < 512 and image_total % (block_rows * 2) == 0:
        block_rows = block_rows * 2
    block_total = image_total // block_rows
    query_blocks = image_qkv[:, :, 0].reshape(block_total, block_rows, local_heads, HEAD)

    def attend(query_block):
        scores = jnp.einsum(
            "qhe,khe->hqk", query_block, keys_all, preferred_element_type=jnp.float32
        ) * HEAD ** (-0.5)
        scores = jnp.where(valid[None, None, :], scores, -1e30)
        row_max = jnp.max(scores, axis=2, keepdims=True)
        weights = jnp.exp(scores - row_max)
        total = jnp.sum(weights, axis=2, keepdims=True)
        probs = weights.astype(jnp.bfloat16)
        mixed = (
            jnp.einsum("hqk,khe->hqe", probs, values_all, preferred_element_type=jnp.float32)
            / total
        )
        return jnp.transpose(mixed.astype(jnp.bfloat16), (1, 0, 2))

    attended = lax.map(attend, query_blocks).reshape(image_total, local_heads * HEAD)
    attended = lax.all_to_all(attended, "seq", split_axis=0, concat_axis=1, tiled=True)
    hidden = image_rows.astype(jnp.float32) + mod_rows[2] * jnp.dot(
        attended, proj_weight, preferred_element_type=jnp.float32
    )
    mlp_norm = modulate(hidden, mod_rows[8], mod_rows[7])
    mlp_all = lax.all_gather(mlp_norm, "seq", axis=0, tiled=True)
    inner = jax.nn.gelu(
        jnp.dot(mlp_all, mlp_in_weight, preferred_element_type=jnp.float32), approximate=True
    ).astype(jnp.bfloat16)
    mlp_out = lax.psum_scatter(
        jnp.dot(inner, mlp_out_weight, preferred_element_type=jnp.float32).astype(jnp.bfloat16),
        "seq",
        scatter_dimension=0,
        tiled=True,
    ).astype(jnp.float32)
    block_out = hidden + mod_rows[9] * mlp_out
    final_norm = modulate(block_out, mod_rows[6], mod_rows[5])
    own_vel = lax.dot_general(
        final_weight, final_norm, (((1,), (1,)), ((), ())), preferred_element_type=jnp.float32
    )
    partner_vel = partner(own_vel.astype(jnp.bfloat16), "cfg", 0).astype(own_vel.dtype)
    leading = lax.axis_index("cfg") == 0
    cond_vel = jnp.where(leading, own_vel, partner_vel)
    uncond_vel = jnp.where(leading, partner_vel, own_vel)
    guided = uncond_vel + guidance[0] * (cond_vel - uncond_vel)
    cond_sq, guided_sq = lax.psum((jnp.sum(cond_vel * cond_vel), jnp.sum(guided * guided)), "seq")
    entries = own_vel.shape[0] * image_total
    rms_cond = jnp.sqrt(cond_sq / entries + EPS_NORM)
    rms_guided = jnp.sqrt(guided_sq / entries + EPS_NORM)
    result_vel = 0.7 * (guided * (rms_cond / rms_guided)) + 0.3 * guided
    channel_half = latents.shape[1]
    channel_start = lax.axis_index("cfg") * channel_half
    own_channels = lax.dynamic_slice_in_dim(result_vel, channel_start, channel_half, 0)
    next_index = jnp.minimum(step_index[0] + step_count[0], STEPS)
    step_size = sigma_of(next_index) - sigma_of(step_index[0])
    moved = latents[0] + step_size * own_channels
    return (own_channels[None], moved[None])


def solution(mesh):
    in_specs = (
        P("cfg", "req", "seq", None),
        P("cfg", "req", "seq", None),
        P("cfg", "req", None, None),
        P(None, "seq"),
        P(),
        P(None, "seq"),
        P("seq", None),
        P(),
        P("req", "cfg", "seq"),
        P("req"),
        P("cfg", "req"),
        P("req"),
        P("req"),
    )
    out_specs = (P("req", "cfg", "seq"), P("req", "cfg", "seq"))
    return jax.shard_map(local, mesh=mesh, in_specs=in_specs, out_specs=out_specs, check_vma=False)
```

profile of v0, /device:TPU:0, one launch (start us, length us, event | category | flops | bytes accessed | tf_op | source)
XLA Modules:
  0.0 482.9 jit_solution(12494964376761365673)
XLA Ops:
  7.2 0.0 copy-start
  7.2 0.0 copy-start.2
  7.2 0.0 all-gather.3.cloned.1.call-start
  7.2 6.5 %copy.24 = bf16[1536,1280]{0,1:T(8,128)(2,1)} copy(bf16[1536,1280]{1,0:T(8,128)(2,1)} %param.16) | data formatting | bytes 7864320 | tf_op args[3]
  13.7 0.0 all-gather.3.cloned.1.call-update
  13.8 1.0 convert_reduce_fusion.1
  14.8 1.6 slice_reduce_fusion.2
  16.4 0.6 copy-done.10
  17.0 1.1 fusion.59
  18.1 0.0 copy-done.2
  18.1 0.1 convert_reduce_fusion
  18.2 0.6 copy-done.9
  18.8 0.3 fusion.31
  19.1 0.6 add_rsqrt_fusion.2
  19.6 0.6 add_rsqrt_fusion.3
  20.2 266.0 %all-gather.3.cloned.1.call-done = bf16[1536,5120]{0,1:T(8,128)(2,1)} async-done(((bf16[1536,1280]{0,1:T(8,128)(2,1)}), bf16[1536,5120]{0,1:T(8,128)(2,1)}) %all-gather.3.cloned.1.call-update) | async-done | bytes 15728656 | tf_op jit(solution)/shard_map/all_gather | solution.py:68
  286.2 6.2 %slice.80 = bf16[1536,16,2,64]{0,3,2,1:T(8,128)(2,1)} slice(bf16[1536,16,5,64]{0,3,2,1:T(8,128)(2,1)} %bitcast.90), slice={[0:1536], [0:16], [3:5], [0:64]} | slice | bytes 12582912 | tf_op jit(solution)/shard_map/slice | solution.py:39
  292.4 8.3 %slice.78 = bf16[1536,16,3,64]{0,3,2,1:T(8,128)(2,1)} slice(bf16[1536,16,5,64]{0,3,2,1:T(8,128)(2,1)} %bitcast.91), slice={[0:1536], [0:16], [0:3], [0:64]} | slice | bytes 18874368 | tf_op jit(solution)/shard_map/slice | solution.py:38
  300.7 4.8 %convolution_convert_fusion.2 = bf16[40,2048]{1,0:T(8,128)(2,1)S(1)} fusion(bf16[1536,2048]{0,1:T(8,128)(2,1)} %bitcast.89, bf16[1,1,40,1536]{3,2,1,0:T(8,128)(2,1)} %param.14, f32[1536]{0:T(1024)} %get-tuple-element.17, f32[1536]{0:T(1024)} %get-tuple-element.24, f32[40]{0:T(128)} %add_rsqrt_fusion.2, f32[40]{0:T(128)} %copy-done.10), kind=kOutput, calls=%fused_computation.20 | convolution fusion | flops 252108800 | bytes 6590784 | tf_op jit(solution)/shard_map/dot_general | solution.py:72
  305.5 0.7 copy.42
  306.2 4.0 all-to-all-start.1
  310.2 7.8 %convolution_convert_fusion = bf16[128,3072]{1,0:T(8,128)(2,1)} fusion(bf16[1536,3072]{0,1:T(8,128)(2,1)} %bitcast.88, bf16[1,1,128,1536]{3,2,1,0:T(8,128)(2,1)S(1)} %copy-done.2, f32[1536]{0:T(1024)} %get-tuple-element.25, f32[1536]{0:T(1024)} %get-tuple-element.26, f32[128]{0:T(128)} %add_rsqrt_fusion.3, f32[128]{0:T(128)} %copy-done.9), kind=kOutput, calls=%fused_computation.6 | convolution fusion | flops 1209532416 | bytes 10630144 | tf_op jit(solution)/shard_map/dot_general | solution.py:69
  318.0 2.3 copy.34
  320.3 0.0 all-to-all-done.1
  320.3 5.1 %all-to-all-start = ((bf16[128,4,768]{0,2,1:T(8,128)(2,1)}), bf16[128,4,768]{0,2,1:T(8,128)(2,1)}, u32[]{:S(2)}, u32[]{:S(2)}) async-start(bf16[128,4,768]{0,2,1:T(8,128)(2,1)} %bitcast.92), calls=%async_computation | async-start | bytes 1572864 | tf_op jit(solution)/shard_map/all_to_all | solution.py:78
  325.4 0.0 all-gather.5.cloned.1.call-start
  326.0 0.6 concatenate.9
  326.6 1.9 reshape.208
  328.5 2.5 fusion.77
  330.9 1.8 copy.39
  332.7 1.8 copy.36
  334.5 11.0 %all-to-all-done = bf16[128,4,768]{0,2,1:T(8,128)(2,1)} async-done(((bf16[128,4,768]{0,2,1:T(8,128)(2,1)}), bf16[128,4,768]{0,2,1:T(8,128)(2,1)}, u32[]{:S(2)}, u32[]{:S(2)}) %all-to-all-start) | async-done | bytes 786464 | tf_op jit(solution)/shard_map/all_to_all | solution.py:78
  345.5 2.6 copy.26
  348.1 2.4 reshape.206
  350.5 1.1 slice_bitcast_fusion.3
  351.5 0.0 copy-start.3
  351.5 2.4 fusion
  353.9 0.0 copy-done.6
  354.0 1.2 fusion.1
  355.1 0.0 copy-done.3
  355.1 2.1 fusion.26
  357.2 1.7 all_to_all.44
  358.9 1.0 copy.33
  359.9 10.8 %all_to_all.51 = bf16[4,128,256]{1,2,0:T(8,128)(2,1)S(1)} all-to-all(bf16[4,128,256]{1,2,0:T(8,128)(2,1)S(1)} %copy.33), channel_id=1, replica_groups=mesh['cfg'=2,'req'=4,'seq'=4] {'seq'}, dimensions={0} | all-to-all | bytes 524288 | tf_op jit(solution)/shard_map/all_to_all | solution.py:109
  370.7 0.0 copy-done
  370.7 1.4 fusion.78
  372.2 0.2 multiply_reduce_fusion.1
  372.4 0.6 copy-done.1
  373.0 0.9 add_convert_fusion.1
  374.0 0.0 all-gather.5.cloned.1.call-update
  374.0 0.0 copy-start.11
  374.0 0.0 reduce-scatter.2.cloned.1.call-start
  374.1 36.1 %all-gather.5.cloned.1.call-done = bf16[512,1536]{1,0:T(8,128)(2,1)} async-done(((bf16[128,1536]{1,0:T(8,128)(2,1)}), bf16[512,1536]{1,0:T(8,128)(2,1)}) %all-gather.5.cloned.1.call-update) | async-done | bytes 1572880 | tf_op jit(solution)/shard_map/all_gather | solution.py:114
  410.2 10.4 %convolution_convert_fusion.1 = bf16[512,1536]{1,0:T(8,128)(2,1)} fusion(bf16[1536,1536]{1,0:T(8,128)(2,1)} %param.19, bf16[512,1536]{1,0:T(8,128)(2,1)} %all-gather.5.cloned.1.call-done, bf16[1536,1536]{1,0:T(8,128)(2,1)} %param.18), kind=kOutput, calls=%fused_computation.15 | convolution fusion | flops 4839702528 | bytes 12582912 | tf_op jit(solution)/shard_map/dot_general | solution.py:119
  420.7 0.0 reduce-scatter.2.cloned.1.call-update
  420.7 34.5 %reduce-scatter.2.cloned.1.call-done = bf16[128,1536]{1,0:T(8,128)(2,1)} async-done(((bf16[512,1536]{1,0:T(8,128)(2,1)}), bf16[128,1536]{1,0:T(8,128)(2,1)}) %reduce-scatter.2.cloned.1.call-update) | async-done | bytes 393232 | tf_op jit(solution)/shard_map/reduce_scatter | solution.py:118
  455.1 1.4 fusion.60
  456.6 1.5 multiply_reduce_fusion
  458.1 1.6 fusion.79
  459.7 1.5 collective-permute-start
  463.3 0.2 collective-permute-done
  463.5 0.6 multiply_reduce_fusion.2
  464.1 10.2 %all-reduce.1 = (f32[]{:T(128)}, f32[]{:T(128)}) all-reduce(f32[]{:T(128)} %get-tuple-element.38, f32[]{:T(128)} %get-tuple-element.32), channel_id=1, replica_groups=mesh['cfg'=2,'req'=4,'seq'=4] {'seq'}, use_global_device_ids=true, to_apply=%region_12.13 | all-reduce | flops 2 | bytes 16 | tf_op jit(solution)/shard_map/psum | solution.py:134
  475.7 0.6 fusion.67
  (20 shorter events, 0.1 us)
Async XLA Ops:
  7.2 363.6 %copy-start = (bf16[1024,1536]{1,0:T(8,128)(2,1)S(1)}, bf16[1024,1536]{1,0:T(8,128)(2,1)}, u32[]{:S(2)}) copy-start(bf16[1024,1536]{1,0:T(8,128)(2,1)} %param.17) | copy-start | bytes 9437188
  7.2 10.9 %copy-start.2 = (bf16[1,1,128,1536]{3,2,1,0:T(8,128)(2,1)S(1)}, bf16[1,1,128,1536]{3,2,1,0:T(8,128)(2,1)}, u32[]{:S(2)}) copy-start(bf16[1,1,128,1536]{3,2,1,0:T(8,128)(2,1)} %param.13) | copy-start | bytes 1179652
  7.2 279.1 %all-gather.3.cloned.1.call-start = ((), (), s32[]{:S(2)}) async-start(), calls=%async_computation.4 | async-start | bytes 19660800 | tf_op jit(solution)/shard_map/all_gather | solution.py:68
  16.4 0.6 copy-start.10
  18.2 0.6 copy-start.9
  306.2 14.1 %all-to-all-start.1 = ((bf16[40,4,512]{2,0,1:T(8,128)(2,1)}), bf16[40,4,512]{2,0,1:T(8,128)(2,1)}, u32[]{:S(2)}, u32[]{:S(2)}) async-start(bf16[40,4,512]{2,0,1:T(8,128)(2,1)} %bitcast.95), calls=%async_computation.1 | async-start | bytes 327680 | tf_op jit(solution)/shard_map/all_to_all | solution.py:79
  320.3 25.1 %all-to-all-start = ((bf16[128,4,768]{0,2,1:T(8,128)(2,1)}), bf16[128,4,768]{0,2,1:T(8,128)(2,1)}, u32[]{:S(2)}, u32[]{:S(2)}) async-start(bf16[128,4,768]{0,2,1:T(8,128)(2,1)} %bitcast.92), calls=%async_computation | async-start | bytes 1572864 | tf_op jit(solution)/shard_map/all_to_all | solution.py:78
  325.4 84.8 %all-gather.5.cloned.1.call-start = ((), (), s32[]{:S(2)}) async-start(), calls=%async_computation.5 | async-start | bytes 1966080 | tf_op jit(solution)/shard_map/all_gather | solution.py:114
  350.4 3.5 copy-start.6
  351.5 3.6 copy-start.3
  358.9 14.1 %copy-start.4 = (f32[1536]{0:T(1024)S(1)}, f32[1536]{0:T(1024)}, u32[]{:S(2)}) copy-start(f32[1536]{0:T(1024)} %get-tuple-element.16) | copy-start | bytes 18436
  372.1 0.9 copy-start.1
  374.0 84.1 %copy-start.7 = (f32[1536]{0:T(1024)S(1)}, f32[1536]{0:T(1024)}, u32[]{:S(2)}) copy-start(f32[1536]{0:T(1024)} %get-tuple-element.28) | copy-start | bytes 18436
  374.0 84.1 %copy-start.8 = (f32[1536]{0:T(1024)S(1)}, f32[1536]{0:T(1024)}, u32[]{:S(2)}) copy-start(f32[1536]{0:T(1024)} %get-tuple-element.29) | copy-start | bytes 18436
  374.0 84.1 %copy-start.11 = (bf16[64,1536]{1,0:T(8,128)(2,1)S(1)}, bf16[64,1536]{1,0:T(8,128)(2,1)}, u32[]{:S(2)}) copy-start(bf16[64,1536]{1,0:T(8,128)(2,1)} %param.20) | copy-start | bytes 589828
  374.0 81.1 %reduce-scatter.2.cloned.1.call-start = ((), (), s32[]{:S(2)}) async-start(), calls=%async_computation.6 | async-start | bytes 1966080 | tf_op jit(solution)/shard_map/reduce_scatter | solution.py:118
  420.6 55.1 %copy-start.5 = (f32[1,32,128]{2,1,0:T(8,128)S(1)}, f32[1,32,128]{2,1,0:T(8,128)}, u32[]{:S(2)}) copy-start(f32[1,32,128]{2,1,0:T(8,128)} %param.21) | copy-start | bytes 49156
  459.7 3.8 collective-permute-start
Sparse Core Ops, SparseCore 0:
  13.9 272.3 all-gather.2
  374.1 36.0 all-gather.4
  420.8 34.2 reduce-scatter.1
where the time goes:
time: 484 us; the launch traced here: 483 us
  waiting for transfers between devices  348 us (72%)
  local copies, waits for them, and re-layouts  42.9 us (9%)
  matrix products  30.6 us (6%)
  blocking collectives  21 us (4%)
  between operations  18 us (4%)
  other arithmetic  11.8 us (2%)
  starting transfers between devices  10.6 us (2%)
    all_gather x1, waiting for transfers between devices, local(): lax.all_gather(attn_weight, 'seq', axis=1, tiled=True)  266 us
    all_gather x1, waiting for transfers between devices, local(): mlp_all = lax.all_gather(mlp_norm, 'seq', axis=0, tiled=True)  36.1 us
    reduce_scatter x1, waiting for transfers between devices, local(): lax.psum_scatter(jnp.dot(inner, mlp_out_weight, preferred_element_type=jn...  34.5 us
    unnamed x27, local copies, waits for them, and re-layouts  11.9 us
    all_to_all x1, waiting for transfers between devices, local(): lax.all_to_all(image_qkv, 'seq', split_axis=1, concat_axis=0, tiled=True)  11 us
    all_to_all x1, blocking collectives, local(): lax.all_to_all(attended, 'seq', split_axis=0, concat_axis=1, tiled=True)  10.8 us
    dot_general x1, matrix products, local(): jnp.dot(inner, mlp_out_weight, preferred_element_type=jnp.float32)  10.4 us
    psum x1, blocking collectives, local(): lax.psum((jnp.sum(cond_vel * cond_vel), jnp.sum(guided * guided)), 'seq')  10.2 us
  transfers between devices with their start and end apart: 6, of which 5 were waited for; matrix products, arithmetic and copies ran while one was open for 5% of the time, Pallas kernels for 0%

commit v1 on v0

--- a/solution.py
+++ b/solution.py
@@ -65,18 +65,15 @@
     text_total = text_rows.shape[0] * seq_size
     image_norm = modulate(image_rows, mod_rows[1], mod_rows[0])
     text_norm = modulate(text_rows, mod_rows[4], mod_rows[3])
-    image_cols, text_cols = split_columns(lax.all_gather(attn_weight, "seq", axis=1, tiled=True))
-    image_part = jnp.dot(image_norm, image_cols, preferred_element_type=jnp.float32).astype(
+    gathered = lax.all_gather(jnp.concatenate([image_norm, text_norm], axis=0), "seq", axis=0)
+    image_all = gathered[:, :local_rows].reshape(image_total, -1)
+    text_all = gathered[:, local_rows:].reshape(text_total, -1)
+    image_cols, text_cols = split_columns(attn_weight)
+    image_qkv = jnp.dot(image_all, image_cols, preferred_element_type=jnp.float32).astype(
         jnp.bfloat16
     )
-    text_part = jnp.dot(text_norm, text_cols, preferred_element_type=jnp.float32).astype(
+    text_kv = jnp.dot(text_all, text_cols, preferred_element_type=jnp.float32).astype(
         jnp.bfloat16
-    )
-    image_qkv = image_part
-    text_kv = text_part
-    image_qkv, text_kv = (
-        lax.all_to_all(image_qkv, "seq", split_axis=1, concat_axis=0, tiled=True),
-        lax.all_to_all(text_kv, "seq", split_axis=1, concat_axis=0, tiled=True),
     )
     image_qkv = image_qkv.reshape(image_total, local_heads, 3, HEAD)
     text_kv = text_kv.reshape(text_total, local_heads, 2, HEAD)

time: 484 us -> 212 us (0.44)
  waiting for transfers between devices: 348 us -> 105 us
  local copies, waits for them, and re-layouts: 42.9 us -> 25.3 us
  starting transfers between devices: 10.6 us -> 1.84 us
  matrix products: 30.6 us -> 23.6 us
    all_gather x1, waiting for transfers between devices: 266 us -> 34.3 us  [local(): lax.all_gather(jnp.concatenate([image_norm, text_norm], axis=0), 'seq', a...]
    all_to_all x2 -> x0, waiting for transfers between devices: 11 us -> none  [the longest x1 11 us: local(): lax.all_to_all(image_qkv, 'seq', split_axis=1, concat_axis=0, tiled=True)]
    all_to_all x2 -> x0, starting transfers between devices: 9.02 us -> none  [the longest x1 5.05 us: local(): lax.all_to_all(image_qkv, 'seq', split_axis=1, concat_axis=0, tiled=True)]
    dot_general x2, matrix products: 12.7 us -> 5.77 us  [the longest x1 4.45 us: local(): jnp.dot(image_all, image_cols, preferred_element_type=jnp.float32)]
    all_to_all x3 -> x0, local copies, waits for them, and re-layouts: 5.59 us -> none  [the longest x2 4.9 us: local(): lax.all_to_all(image_qkv, 'seq', split_axis=1, concat_axis=0, tiled=True)]
    unnamed x27 -> x25, local copies, waits for them, and re-layouts: 11.9 us -> 6.96 us
    slice x1, local copies, waits for them, and re-layouts: 8.28 us -> 3.39 us  [split_columns(): image_cols = shaped[:, :, 0:3, :].reshape(width_in, head_count * 3 * HEAD)]
  transfers between devices with their start and end apart: 6 -> 4, of which waited for: 5 -> 4; matrix products, arithmetic and copies ran while one was open for 5% -> 6% of each run, Pallas kernels for 0% -> 0%
where the time goes in v1:
time: 212 us; the launch traced here: 211 us
  waiting for transfers between devices  105 us (50%)
  local copies, waits for them, and re-layouts  25.3 us (12%)
  matrix products  23.6 us (11%)
  blocking collectives  21.7 us (10%)
  between operations  18 us (8%)
  other arithmetic  15.9 us (8%)
    all_gather x1, waiting for transfers between devices, local(): mlp_all = lax.all_gather(mlp_norm, 'seq', axis=0, tiled=True)  35.9 us
    reduce_scatter x1, waiting for transfers between devices, local(): lax.psum_scatter(jnp.dot(inner, mlp_out_weight, preferred_element_type=jn...  34.5 us
    all_gather x1, waiting for transfers between devices, local(): lax.all_gather(jnp.concatenate([image_norm, text_norm], axis=0), 'seq', a...  34.3 us
    all_to_all x1, blocking collectives, local(): lax.all_to_all(attended, 'seq', split_axis=0, concat_axis=1, tiled=True)  11.5 us
    dot_general x1, matrix products, local(): jnp.dot(inner, mlp_out_weight, preferred_element_type=jnp.float32)  10.4 us
    psum x1, blocking collectives, local(): lax.psum((jnp.sum(cond_vel * cond_vel), jnp.sum(guided * guided)), 'seq')  10.2 us
    unnamed x25, local copies, waits for them, and re-layouts  6.96 us
    dot_general x1, matrix products, local(): jnp.dot(image_all, image_cols, preferred_element_type=jnp.float32)  4.45 us
  transfers between devices with their start and end apart: 4, of which 4 were waited for; matrix products, arithmetic and copies ran while one was open for 6% of the time, Pallas kernels for 0%

profile of v1, /device:TPU:0, one launch (start us, length us, event | category | flops | bytes accessed | tf_op | source)
XLA Modules:
  0.0 211.3 jit_solution(18187217547480818482)
XLA Ops:
  7.2 0.0 copy-start
  7.2 0.0 all-gather.6.cloned.1.call-start
  7.2 1.7 slice_reduce_fusion.2
  9.0 1.0 convert_reduce_fusion.1
  10.0 1.1 fusion.50
  11.1 1.1 convert_reduce_fusion
  12.3 1.2 fusion.32
  13.5 1.0 fusion.53
  14.5 1.3 fusion.35
  15.8 0.8 pad_maximum_fusion
  16.7 0.0 all-gather.6.cloned.1.call-update
  16.7 0.0 all-gather.4.cloned.1.call-start
  16.7 6.3 %copy.20 = bf16[1536,1280]{0,1:T(8,128)(2,1)} copy(bf16[1536,1280]{1,0:T(8,128)(2,1)} %param.16) | data formatting | bytes 7864320 | tf_op args[3]
  23.0 2.8 %slice.90 = bf16[1536,4,2,64]{0,3,2,1:T(8,128)(2,1)} slice(bf16[1536,4,5,64]{0,3,2,1:T(8,128)(2,1)} %bitcast.102), slice={[0:1536], [0:4], [3:5], [0:64]} | slice | bytes 3145728 | tf_op jit(solution)/shard_map/slice | solution.py:39
  25.8 3.4 %slice.87 = bf16[1536,4,3,64]{0,3,2,1:T(8,128)(2,1)} slice(bf16[1536,4,5,64]{0,3,2,1:T(8,128)(2,1)} %bitcast.103), slice={[0:1536], [0:4], [0:3], [0:64]} | slice | bytes 4718592 | tf_op jit(solution)/shard_map/slice | solution.py:38
  29.8 0.6 concatenate.12
  30.4 34.3 %all-gather.6.cloned.1.call-done = bf16[672,1536]{1,0:T(8,128)(2,1)} async-done(((bf16[168,1536]{1,0:T(8,128)(2,1)}), bf16[672,1536]{1,0:T(8,128)(2,1)}) %all-gather.6.cloned.1.call-update) | async-done | bytes 2064400 | tf_op jit(solution)/shard_map/all_gather | solution.py:68
  64.7 0.0 copy-start.2
  64.7 1.2 slice.89
  65.9 2.7 %slice.86 = bf16[4,128,1536]{2,1,0:T(8,128)(2,1)} slice(bf16[4,168,1536]{2,1,0:T(8,128)(2,1)} %bitcast.109), slice={[0:4], [0:128], [0:1536]} | slice | bytes 3145728 | tf_op jit(solution)/shard_map/slice | solution.py:69
  68.5 0.0 copy-done.2
  68.6 1.3 convolution_convert_fusion.2
  69.9 1.0 copy.24
  70.9 0.7 slice_bitcast_fusion.5
  71.6 4.5 %convolution_convert_fusion.1 = bf16[512,768]{1,0:T(8,128)(2,1)} fusion(bf16[512,1536]{1,0:T(8,128)(2,1)} %bitcast.111, bf16[1536,768]{0,1:T(8,128)(2,1)} %bitcast.107), kind=kOutput, calls=%fused_computation.23 | convolution fusion | flops 1208352768 | bytes 4718592 | tf_op jit(solution)/shard_map/dot_general | solution.py:72
  76.0 2.3 %copy.21 = bf16[512,768]{0,1:T(8,128)(2,1)} copy(bf16[512,768]{1,0:T(8,128)(2,1)} %convolution_convert_fusion.1) | data formatting | bytes 1572864 | tf_op jit(solution)/shard_map/convert_element_type | solution.py:72
  78.3 1.1 slice_bitcast_fusion.3
  79.4 0.0 copy-done.7
  79.4 2.3 %fusion = (f32[4,512]{1,0:T(4,128)S(1)}, f32[4,512,672]{1,2,0:T(8,128)S(1)}) fusion(pred[672]{0:T(1024)(128)(4,1)S(1)} %copy-done.7, bf16[160,4,64]{0,2,1:T(8,128)(2,1)S(1)} %get-tuple-element.37, bf16[512,4,64]{0,2,1:T(8,128)(2,1)S(1)} %get-tuple-element.35, bf16[512,4,3,64]{0,3,2,1:T(8,128)(2,1)} %bitcast.106), kind=kOutput, calls=%fused_computation.2 | convolution fusion | flops 180975616 | bytes 6120096 | tf_op jit(solution)/shard_map/while/body/eval_jaxpr/qhe,khe->hqk/dot_general | solution.py:91
  81.7 0.0 copy-start.4
  81.7 0.0 copy-start.8
  81.8 1.2 fusion.1
  82.9 0.0 copy-done.4
  82.9 0.0 copy-done.8
  82.9 0.0 copy-start.3
  83.0 2.1 fusion.26
  85.0 1.7 all_to_all.14
  86.7 1.0 copy.28
  87.8 11.5 %all_to_all.19 = bf16[4,128,256]{1,2,0:T(8,128)(2,1)S(1)} all-to-all(bf16[4,128,256]{1,2,0:T(8,128)(2,1)S(1)} %copy.28), channel_id=1, replica_groups=mesh['cfg'=2,'req'=4,'seq'=4] {'seq'}, dimensions={0} | all-to-all | bytes 524288 | tf_op jit(solution)/shard_map/all_to_all | solution.py:106
  99.2 0.0 copy-done
  99.2 0.0 copy-done.3
  99.2 1.4 fusion.65
  100.6 0.2 multiply_reduce_fusion.1
  100.9 0.6 copy-done.1
  101.5 0.0 copy-done.5
  101.5 0.9 add_convert_fusion.1
  102.5 0.0 all-gather.4.cloned.1.call-update
  102.5 0.2 reduce-scatter.2.cloned.1.call-start
  102.7 35.9 %all-gather.4.cloned.1.call-done = bf16[512,1536]{1,0:T(8,128)(2,1)} async-done(((bf16[128,1536]{1,0:T(8,128)(2,1)}), bf16[512,1536]{1,0:T(8,128)(2,1)}) %all-gather.4.cloned.1.call-update) | async-done | bytes 1572880 | tf_op jit(solution)/shard_map/all_gather | solution.py:111
  138.6 10.4 %convolution_convert_fusion = bf16[512,1536]{1,0:T(8,128)(2,1)} fusion(bf16[1536,1536]{1,0:T(8,128)(2,1)} %param.19, bf16[512,1536]{1,0:T(8,128)(2,1)} %all-gather.4.cloned.1.call-done, bf16[1536,1536]{1,0:T(8,128)(2,1)} %param.18), kind=kOutput, calls=%fused_computation.14 | convolution fusion | flops 4839702528 | bytes 12582912 | tf_op jit(solution)/shard_map/dot_general | solution.py:116
  149.0 0.0 reduce-scatter.2.cloned.1.call-update
  149.1 34.5 %reduce-scatter.2.cloned.1.call-done = bf16[128,1536]{1,0:T(8,128)(2,1)} async-done(((bf16[512,1536]{1,0:T(8,128)(2,1)}), bf16[128,1536]{1,0:T(8,128)(2,1)}) %reduce-scatter.2.cloned.1.call-update) | async-done | bytes 393232 | tf_op jit(solution)/shard_map/reduce_scatter | solution.py:115
  183.5 1.4 fusion.54
  184.9 1.5 multiply_reduce_fusion
  186.4 0.0 copy-done.9
  186.4 0.0 copy-done.10
  186.5 0.0 copy-done.11
  186.5 1.6 fusion.66
  188.1 1.5 collective-permute-start
  191.7 0.2 collective-permute-done
  191.9 0.6 multiply_reduce_fusion.2
  192.5 10.2 %all-reduce.1 = (f32[]{:T(128)}, f32[]{:T(128)}) all-reduce(f32[]{:T(128)} %get-tuple-element.38, f32[]{:T(128)} %get-tuple-element.32), channel_id=1, replica_groups=mesh['cfg'=2,'req'=4,'seq'=4] {'seq'}, use_global_device_ids=true, to_apply=%region_12.13 | all-reduce | flops 2 | bytes 16 | tf_op jit(solution)/shard_map/psum | solution.py:131
  204.1 0.0 copy-done.6
  204.1 0.6 fusion.55
  (16 shorter events, 0.1 us)
Async XLA Ops:
  7.2 92.1 %copy-start = (bf16[1024,1536]{1,0:T(8,128)(2,1)S(1)}, bf16[1024,1536]{1,0:T(8,128)(2,1)}, u32[]{:S(2)}) copy-start(bf16[1024,1536]{1,0:T(8,128)(2,1)} %param.17) | copy-start | bytes 9437188
  7.2 57.5 %all-gather.6.cloned.1.call-start = ((), (), s32[]{:S(2)}) async-start(), calls=%async_computation.4 | async-start | bytes 2580480 | tf_op jit(solution)/shard_map/all_gather | solution.py:68
  16.7 121.9 %all-gather.4.cloned.1.call-start = ((), (), s32[]{:S(2)}) async-start(), calls=%async_computation.2 | async-start | bytes 1966080 | tf_op jit(solution)/shard_map/all_gather | solution.py:111
  64.7 3.9 %copy-start.2 = (bf16[1536,4,2,64]{0,3,2,1:T(8,128)(2,1)S(1)}, bf16[1536,4,2,64]{0,3,2,1:T(8,128)(2,1)}, u32[]{:S(2)}) copy-start(bf16[1536,4,2,64]{0,3,2,1:T(8,128)(2,1)} %slice.90) | copy-start | bytes 4718596
  71.6 7.8 %copy-start.7 = (pred[672]{0:T(1024)(128)(4,1)S(1)}, pred[672]{0:T(1024)(128)(4,1)}, u32[]{:S(2)}) copy-start(pred[672]{0:T(1024)(128)(4,1)} %concatenate.12) | copy-start | bytes 2020
  81.7 1.2 copy-start.4
  81.7 1.2 copy-start.8
  82.9 16.3 %copy-start.3 = (bf16[1,1,128,1536]{3,2,1,0:T(8,128)(2,1)S(1)}, bf16[1,1,128,1536]{3,2,1,0:T(8,128)(2,1)}, u32[]{:S(2)}) copy-start(bf16[1,1,128,1536]{3,2,1,0:T(8,128)(2,1)} %param.13) | copy-start | bytes 1179652
  86.7 14.8 %copy-start.5 = (f32[1536]{0:T(1024)S(1)}, f32[1536]{0:T(1024)}, u32[]{:S(2)}) copy-start(f32[1536]{0:T(1024)} %get-tuple-element.16) | copy-start | bytes 18436
  100.6 0.9 copy-start.1
  102.5 81.0 %reduce-scatter.2.cloned.1.call-start = ((), (), s32[]{:S(2)}) async-start(), calls=%async_computation.3 | async-start | bytes 1966080 | tf_op jit(solution)/shard_map/reduce_scatter | solution.py:115
  149.0 37.4 %copy-start.9 = (f32[1536]{0:T(1024)S(1)}, f32[1536]{0:T(1024)}, u32[]{:S(2)}) copy-start(f32[1536]{0:T(1024)} %get-tuple-element.28) | copy-start | bytes 18436
  149.0 37.4 %copy-start.10 = (f32[1536]{0:T(1024)S(1)}, f32[1536]{0:T(1024)}, u32[]{:S(2)}) copy-start(f32[1536]{0:T(1024)} %get-tuple-element.29) | copy-start | bytes 18436
  149.0 37.4 %copy-start.11 = (bf16[64,1536]{1,0:T(8,128)(2,1)S(1)}, bf16[64,1536]{1,0:T(8,128)(2,1)}, u32[]{:S(2)}) copy-start(bf16[64,1536]{1,0:T(8,128)(2,1)} %param.20) | copy-start | bytes 589828
  149.0 55.1 %copy-start.6 = (f32[1,32,128]{2,1,0:T(8,128)S(1)}, f32[1,32,128]{2,1,0:T(8,128)}, u32[]{:S(2)}) copy-start(f32[1,32,128]{2,1,0:T(8,128)} %param.21) | copy-start | bytes 49156
  188.1 3.8 %collective-permute-start = (bf16[64,128]{1,0:T(8,128)(2,1)S(1)}, bf16[64,128]{1,0:T(8,128)(2,1)S(1)}, u32[]{:S(2)}, u32[]{:S(2)}) collective-permute-start(bf16[64,128]{1,0:T(8,128)(2,1)S(1)} %get-tuple-element.45), channel_id=1, source_target_pairs={{0,16},{16,0},{1,17},{17,1},{2,18},{18,2},{3,19},{19,3},{4,20},{20... | collective-permute-start | bytes 49160 | tf_op jit(solution)/shard_map/ppermute | solution.py:17
Sparse Core Ops, SparseCore 0:
  16.8 47.8 all-gather.5
  102.6 35.9 all-gather.3
  149.2 34.2 reduce-scatter.1

commit v2 on v1

--- a/solution.py
+++ b/solution.py
@@ -15,6 +15,11 @@
     mask = 2**distance
     pairs = [(source, source ^ mask) for source in range(lax.axis_size(axis))]
     return lax.ppermute(value, axis, pairs)
+
+
+def shifted(value, axis, shift):
+    size = lax.axis_size(axis)
+    return lax.ppermute(value, axis, [(source, (source - shift) % size) for source in range(size)])
 
 
 def modulate(rows_in, scale_row, shift_row):
@@ -65,7 +70,9 @@
     text_total = text_rows.shape[0] * seq_size
     image_norm = modulate(image_rows, mod_rows[1], mod_rows[0])
     text_norm = modulate(text_rows, mod_rows[4], mod_rows[3])
-    gathered = lax.all_gather(jnp.concatenate([image_norm, text_norm], axis=0), "seq", axis=0)
+    seq_index = lax.axis_index("seq")
+    own_norm = jnp.concatenate([image_norm, text_norm], axis=0)
+    gathered = jnp.stack([own_norm] + [shifted(own_norm, "seq", k) for k in range(1, seq_size)])
     image_all = gathered[:, :local_rows].reshape(image_total, -1)
     text_all = gathered[:, local_rows:].reshape(text_total, -1)
     image_cols, text_cols = split_columns(attn_weight)
@@ -79,7 +86,9 @@
     text_kv = text_kv.reshape(text_total, local_heads, 2, HEAD)
     keys_all = jnp.concatenate([image_qkv[:, :, 1], text_kv[:, :, 0]], axis=0)
     values_all = jnp.concatenate([image_qkv[:, :, 2], text_kv[:, :, 1]], axis=0)
-    slots = jnp.arange(text_total, dtype=jnp.int32)
+    text_local = text_rows.shape[0]
+    sources = (seq_index + jnp.arange(seq_size, dtype=jnp.int32)) % seq_size
+    slots = (sources[:, None] * text_local + jnp.arange(text_local, dtype=jnp.int32)).reshape(-1)
     valid = jnp.concatenate([jnp.ones((image_total,), dtype=bool), slots < text_lengths[0, 0]])
     block_rows = local_rows
     while block_rows < 512 and image_total % (block_rows * 2) == 0:
@@ -103,21 +112,28 @@
         return jnp.transpose(mixed.astype(jnp.bfloat16), (1, 0, 2))
 
     attended = lax.map(attend, query_blocks).reshape(image_total, local_heads * HEAD)
-    attended = lax.all_to_all(attended, "seq", split_axis=0, concat_axis=1, tiled=True)
-    hidden = image_rows.astype(jnp.float32) + mod_rows[2] * jnp.dot(
-        attended, proj_weight, preferred_element_type=jnp.float32
-    )
+    attended = attended.reshape(seq_size, local_rows, local_heads * HEAD)
+    head_width = local_heads * HEAD
+    projected = jnp.zeros((local_rows, proj_weight.shape[1]), jnp.float32)
+    for k in range(seq_size):
+        piece = attended[k] if k == 0 else shifted(attended[k], "seq", -k)
+        rows = lax.dynamic_slice_in_dim(
+            proj_weight, ((seq_index - k) % seq_size) * head_width, head_width, 0
+        )
+        projected = projected + jnp.dot(piece, rows, preferred_element_type=jnp.float32)
+    hidden = image_rows.astype(jnp.float32) + mod_rows[2] * projected
     mlp_norm = modulate(hidden, mod_rows[8], mod_rows[7])
-    mlp_all = lax.all_gather(mlp_norm, "seq", axis=0, tiled=True)
-    inner = jax.nn.gelu(
-        jnp.dot(mlp_all, mlp_in_weight, preferred_element_type=jnp.float32), approximate=True
-    ).astype(jnp.bfloat16)
-    mlp_out = lax.psum_scatter(
-        jnp.dot(inner, mlp_out_weight, preferred_element_type=jnp.float32).astype(jnp.bfloat16),
-        "seq",
-        scatter_dimension=0,
-        tiled=True,
-    ).astype(jnp.float32)
+    mlp_out = jnp.zeros((local_rows, mlp_out_weight.shape[1]), jnp.float32)
+    for k in range(seq_size):
+        piece = mlp_norm if k == 0 else shifted(mlp_norm, "seq", k)
+        inner = jax.nn.gelu(
+            jnp.dot(piece, mlp_in_weight, preferred_element_type=jnp.float32), approximate=True
+        ).astype(jnp.bfloat16)
+        part = jnp.dot(inner, mlp_out_weight, preferred_element_type=jnp.float32).astype(
+            jnp.bfloat16
+        )
+        part = part if k == 0 else shifted(part, "seq", -k)
+        mlp_out = mlp_out + part.astype(jnp.float32)
     block_out = hidden + mod_rows[9] * mlp_out
     final_norm = modulate(block_out, mod_rows[6], mod_rows[5])
     own_vel = lax.dot_general(
@@ -128,7 +144,10 @@
     cond_vel = jnp.where(leading, own_vel, partner_vel)
     uncond_vel = jnp.where(leading, partner_vel, own_vel)
     guided = uncond_vel + guidance[0] * (cond_vel - uncond_vel)
-    cond_sq, guided_sq = lax.psum((jnp.sum(cond_vel * cond_vel), jnp.sum(guided * guided)), "seq")
+    squares = jnp.stack([jnp.sum(cond_vel * cond_vel), jnp.sum(guided * guided)])
+    for bit in range(seq_size.bit_length() - 1):
+        squares = squares + partner(squares, "seq", bit)
+    cond_sq, guided_sq = squares[0], squares[1]
     entries = own_vel.shape[0] * image_total
     rms_cond = jnp.sqrt(cond_sq / entries + EPS_NORM)
     rms_guided = jnp.sqrt(guided_sq / entries + EPS_NORM)

time: 212 us -> 199 us (0.939)
  starting transfers between devices: 1.84 us -> 50.2 us
  waiting for transfers between devices: 105 us -> 61.2 us
  blocking collectives: 21.7 us -> 0 us
  matrix products: 23.6 us -> 37.9 us
  between operations: 18 us -> 5 us
  other arithmetic: 15.9 us -> 22 us
  local copies, waits for them, and re-layouts: 25.3 us -> 21.5 us
    all_gather x2 -> x0, waiting for transfers between devices: 70.1 us -> none  [the longest x1 35.9 us: local(): mlp_all = lax.all_gather(mlp_norm, 'seq', axis=0, tiled=True)]
    ppermute x0 -> x12, waiting for transfers between devices: none -> 53.7 us  [shifted(): lax.ppermute(value, axis, [(source, (source - shift) % size) for source i...]
    ppermute x0 -> x12, starting transfers between devices: none -> 47.9 us  [shifted(): lax.ppermute(value, axis, [(source, (source - shift) % size) for source i...]
    reduce_scatter x1 -> x0, waiting for transfers between devices: 34.5 us -> none  [local(): lax.psum_scatter(jnp.dot(inner, mlp_out_weight, preferred_element_type=jn...]
    dot_general x1 -> x4, matrix products: 10.4 us -> 26.1 us  [local(): jnp.dot(inner, mlp_out_weight, preferred_element_type=jnp.float32)]
    all_to_all x1 -> x0, blocking collectives: 11.5 us -> none  [local(): lax.all_to_all(attended, 'seq', split_axis=0, concat_axis=1, tiled=True)]
    psum x1 -> x0, blocking collectives: 10.2 us -> none  [local(): lax.psum((jnp.sum(cond_vel * cond_vel), jnp.sum(guided * guided)), 'seq')]
    ppermute x1 -> x3, waiting for transfers between devices: 0.22 us -> 7.49 us  [partner(): return lax.ppermute(value, axis, pairs)]
  transfers between devices with their start and end apart: 4 -> 15, of which waited for: 4 -> 9; matrix products, arithmetic and copies ran while one was open for 6% -> 17% of each run, Pallas kernels for 0% -> 0%
where the time goes in v2:
time: 199 us; the launch traced here: 198 us
  waiting for transfers between devices  61.2 us (31%)
  starting transfers between devices  50.2 us (25%)
  matrix products  37.9 us (19%)
  other arithmetic  22 us (11%)
  local copies, waits for them, and re-layouts  21.5 us (11%)
  between operations  5 us (3%)
    ppermute x12, waiting for transfers between devices, shifted(): lax.ppermute(value, axis, [(source, (source - shift) % size) for source i...  53.7 us
    ppermute x12, starting transfers between devices, shifted(): lax.ppermute(value, axis, [(source, (source - shift) % size) for source i...  47.9 us
    dot_general x4, matrix products, local(): jnp.dot(inner, mlp_out_weight, preferred_element_type=jnp.float32)  26.1 us
    unnamed x35, local copies, waits for them, and re-layouts  7.69 us
    ppermute x3, waiting for transfers between devices, partner(): return lax.ppermute(value, axis, pairs)  7.49 us
    another operation x2, other arithmetic, local(): jnp.stack([own_norm] + [shifted(own_norm, 'seq', k) for k in range(1, seq...  4.14 us
  transfers between devices with their start and end apart: 15, of which 9 were waited for; matrix products, arithmetic and copies ran while one was open for 17% of the time, Pallas kernels for 0%

profile of v2, /device:TPU:0, one launch (start us, length us, event | category | flops | bytes accessed | tf_op | source)
XLA Modules:
  0.0 197.8 jit_solution(8743713805965781177)
XLA Ops:
  0.6 1.7 add_reduce_fusion
  2.4 1.0 convert_reduce_fusion.1
  3.4 1.1 fusion.100
  4.5 1.1 convert_reduce_fusion
  5.7 1.2 fusion.22
  6.9 1.0 fusion.103
  8.0 1.3 fusion.25
  9.3 1.0 fusion.132
  10.3 3.1 %collective-permute-start.2 = (bf16[168,1536]{1,0:T(8,128)(2,1)}, bf16[168,1536]{1,0:T(8,128)(2,1)}, u32[]{:S(2)}, u32[]{:S(2)}) collective-permute-start(bf16[168,1536]{1,0:T(8,128)(2,1)} %get-tuple-element.35), channel_id=1, source_target_pairs={{0,1},{1,2},{2,3},{3,0},{4,5},{5,6},{6,7},{7,4},{8,9},{9,10},{10,1... | collective-permute-start | bytes 1548296 | tf_op jit(solution)/shard_map/ppermute | solution.py:22
  13.4 2.6 %collective-permute-start.1 = (bf16[168,1536]{1,0:T(8,128)(2,1)}, bf16[168,1536]{1,0:T(8,128)(2,1)}, u32[]{:S(2)}, u32[]{:S(2)}) collective-permute-start(bf16[168,1536]{1,0:T(8,128)(2,1)} %get-tuple-element.35), channel_id=1, source_target_pairs={{0,2},{1,3},{2,0},{3,1},{4,6},{5,7},{6,4},{7,5},{8,10},{9,11},{10,... | collective-permute-start | bytes 1548296 | tf_op jit(solution)/shard_map/ppermute | solution.py:22
  16.0 1.3 collective-permute-start
  17.3 6.3 %copy.20 = bf16[1536,1280]{0,1:T(8,128)(2,1)} copy(bf16[1536,1280]{1,0:T(8,128)(2,1)} %param.16) | data formatting | bytes 7864320 | tf_op args[3]
  23.6 2.7 %slice.117 = bf16[1536,4,2,64]{0,3,2,1:T(8,128)(2,1)} slice(bf16[1536,4,5,64]{0,3,2,1:T(8,128)(2,1)} %bitcast.119), slice={[0:1536], [0:4], [3:5], [0:64]} | slice | bytes 3145728 | tf_op jit(solution)/shard_map/slice | solution.py:44
  26.2 3.2 %slice.115 = bf16[1536,4,3,64]{0,3,2,1:T(8,128)(2,1)} slice(bf16[1536,4,5,64]{0,3,2,1:T(8,128)(2,1)} %bitcast.120), slice={[0:1536], [0:4], [0:3], [0:64]} | slice | bytes 4718592 | tf_op jit(solution)/shard_map/slice | solution.py:43
  30.3 0.6 concatenate.12
  30.9 18.8 %collective-permute-done.1 = bf16[168,1536]{1,0:T(8,128)(2,1)} collective-permute-done((bf16[168,1536]{1,0:T(8,128)(2,1)}, bf16[168,1536]{1,0:T(8,128)(2,1)}, u32[]{:S(2)}, u32[]{:S(2)}) %collective-permute-start.1) | collective-permute-done | bytes 516128 | tf_op jit(solution)/shard_map/ppermute | solution.py:22
  49.7 1.1 pad_maximum_fusion.2
  50.8 3.1 %pad_maximum_fusion = bf16[4,168,1536]{2,1,0:T(8,128)(2,1)} fusion(bf16[1,168,1536]{2,1,0:T(8,128)(2,1)} %bitcast.6, bf16[1,168,1536]{2,1,0:T(8,128)(2,1)} %bitcast.5, bf16[1,168,1536]{2,1,0:T(8,128)(2,1)} %bitcast.4, bf16[1,168,1536]{2,1,0:T(8,128)(2,1)} %get-tuple-element.34), kind=kLoop, calls=%fused_computation.17 | loop fusion | flops 3096576 | bytes 4128768 | tf_op jit(solution)/shard_map/stack | solution.py:75
  53.9 1.3 convolution_convert_fusion.5
  55.3 1.0 copy.24
  56.3 0.7 slice_bitcast_fusion.5
  57.0 1.5 slice.114
  58.5 4.0 %convolution_convert_fusion.4 = bf16[512,768]{1,0:T(8,128)(2,1)} fusion(bf16[512,1536]{1,0:T(8,128)(2,1)S(1)} %bitcast.126, bf16[1536,768]{0,1:T(8,128)(2,1)} %bitcast.124), kind=kOutput, calls=%fused_computation.18 | convolution fusion | flops 1208352768 | bytes 4718592 | tf_op jit(solution)/shard_map/dot_general | solution.py:79
  62.5 2.3 %copy.21 = bf16[512,768]{0,1:T(8,128)(2,1)} copy(bf16[512,768]{1,0:T(8,128)(2,1)} %convolution_convert_fusion.4) | data formatting | bytes 1572864 | tf_op jit(solution)/shard_map/convert_element_type | solution.py:79
  64.8 1.1 slice_bitcast_fusion.3
  65.9 2.4 %fusion = (f32[4,512]{1,0:T(4,128)S(1)}, f32[4,512,672]{1,2,0:T(8,128)S(1)}) fusion(pred[672]{0:T(1024)(128)(4,1)S(1)} %copy-done.7, bf16[160,4,64]{0,2,1:T(8,128)(2,1)S(1)} %get-tuple-element.41, bf16[512,4,64]{0,2,1:T(8,128)(2,1)S(1)} %get-tuple-element.33, bf16[512,4,3,64]{0,3,2,1:T(8,128)(2,1)} %bitcast.123), kind=kOutput, calls=%fused_computation.2 | convolution fusion | flops 180975616 | bytes 6120096 | tf_op jit(solution)/shard_map/while/body/eval_jaxpr/qhe,khe->hqk/dot_general | solution.py:100
  68.2 1.2 fusion.1
  69.4 1.4 fusion.16
  70.9 12.6 %collective-permute-start.5 = (bf16[128,256]{0,1:T(8,128)(2,1)S(1)}, bf16[128,256]{0,1:T(8,128)(2,1)S(1)}, u32[]{:S(2)}, u32[]{:S(2)}) collective-permute-start(bf16[128,256]{0,1:T(8,128)(2,1)S(1)} %bitcast.130), channel_id=1, source_target_pairs={{0,3},{1,0},{2,1},{3,2},{4,7},{5,4},{6,5},{7,6},{8,11},{9,8},{10,9... | collective-permute-start | bytes 196616 | tf_op jit(solution)/shard_map/ppermute | solution.py:22
  83.5 0.6 collective-permute-start.4
  84.1 0.3 fusion.62
  84.4 5.2 %collective-permute-done.3 = bf16[128,256]{0,1:T(8,128)(2,1)S(1)} collective-permute-done((bf16[128,256]{0,1:T(8,128)(2,1)S(1)}, bf16[128,256]{0,1:T(8,128)(2,1)S(1)}, u32[]{:S(2)}, u32[]{:S(2)}) %collective-permute-start.3) | collective-permute-done | bytes 65568 | tf_op jit(solution)/shard_map/ppermute | solution.py:22
  89.6 0.3 convolution_add_fusion.1
  89.9 0.3 fusion.58
  90.3 0.4 fusion.135
  90.8 0.2 multiply_reduce_fusion.1
  91.0 0.6 copy-done.1
  91.7 0.2 add_convert_fusion.1
  91.9 0.6 collective-permute-start.10
  92.5 2.1 %collective-permute-start.8 = (bf16[128,1536]{1,0:T(8,128)(2,1)S(1)}, bf16[128,1536]{1,0:T(8,128)(2,1)}, u32[]{:S(2)}, u32[]{:S(2)}) collective-permute-start(bf16[128,1536]{1,0:T(8,128)(2,1)S(1)} %add_convert_fusion.1), channel_id=1, source_target_pairs={{0,2},{1,3},{2,0},{3,1},{4,6},{5,7},{6,4},{7,5},{8,10},{9,11},{10,... | collective-permute-start | bytes 1179656 | tf_op jit(solution)/shard_map/ppermute | solution.py:22
  94.6 1.3 collective-permute-start.6
  95.9 10.0 %collective-permute-done.10 = bf16[128,1536]{1,0:T(8,128)(2,1)} collective-permute-done((bf16[128,1536]{1,0:T(8,128)(2,1)S(1)}, bf16[128,1536]{1,0:T(8,128)(2,1)}, u32[]{:S(2)}, u32[]{:S(2)}) %collective-permute-start.10) | collective-permute-done | bytes 393248 | tf_op jit(solution)/shard_map/ppermute | solution.py:22
  105.9 6.3 %convolution_convert_fusion = bf16[128,1536]{1,0:T(8,128)(2,1)} fusion(bf16[1536,1536]{1,0:T(8,128)(2,1)} %param.19, bf16[128,1536]{1,0:T(8,128)(2,1)} %collective-permute-done.10, bf16[1536,1536]{1,0:T(8,128)(2,1)} %param.18), kind=kOutput, calls=%fused_computation.12 | convolution fusion | flops 1209925632 | bytes 10223616 | tf_op jit(solution)/shard_map/dot_general | solution.py:132
  112.2 0.8 collective-permute-start.11
  113.0 7.1 %collective-permute-done.8 = bf16[128,1536]{1,0:T(8,128)(2,1)} collective-permute-done((bf16[128,1536]{1,0:T(8,128)(2,1)S(1)}, bf16[128,1536]{1,0:T(8,128)(2,1)}, u32[]{:S(2)}, u32[]{:S(2)}) %collective-permute-start.8) | collective-permute-done | bytes 393248 | tf_op jit(solution)/shard_map/ppermute | solution.py:22
  120.0 6.3 %convolution_convert_fusion.1 = bf16[128,1536]{1,0:T(8,128)(2,1)} fusion(bf16[1536,1536]{1,0:T(8,128)(2,1)} %param.19, bf16[128,1536]{1,0:T(8,128)(2,1)} %collective-permute-done.8, bf16[1536,1536]{1,0:T(8,128)(2,1)} %param.18), kind=kOutput, calls=%fused_computation.13 | convolution fusion | flops 1209925632 | bytes 10223616 | tf_op jit(solution)/shard_map/dot_general | solution.py:132
  126.3 20.8 %collective-permute-start.9 = (bf16[128,1536]{1,0:T(8,128)(2,1)}, bf16[128,1536]{1,0:T(8,128)(2,1)}, u32[]{:S(2)}, u32[]{:S(2)}) collective-permute-start(bf16[128,1536]{1,0:T(8,128)(2,1)} %convolution_convert_fusion.1), channel_id=1, source_target_pairs={{0,2},{1,3},{2,0},{3,1},{4,6},{5,7},{6,4},{7,5},{8,10},{9,11},{10,... | collective-permute-start | bytes 1179656 | tf_op jit(solution)/shard_map/ppermute | solution.py:22
  147.2 6.3 %convolution_convert_fusion.2 = bf16[128,1536]{1,0:T(8,128)(2,1)} fusion(bf16[1536,1536]{1,0:T(8,128)(2,1)} %param.19, bf16[128,1536]{1,0:T(8,128)(2,1)} %collective-permute-done.6, bf16[1536,1536]{1,0:T(8,128)(2,1)} %param.18), kind=kOutput, calls=%fused_computation.14 | convolution fusion | flops 1209925632 | bytes 10223616 | tf_op jit(solution)/shard_map/dot_general | solution.py:132
  153.5 2.0 %collective-permute-start.7 = (bf16[128,1536]{1,0:T(8,128)(2,1)}, bf16[128,1536]{1,0:T(8,128)(2,1)S(1)}, u32[]{:S(2)}, u32[]{:S(2)}) collective-permute-start(bf16[128,1536]{1,0:T(8,128)(2,1)} %convolution_convert_fusion.2), channel_id=1, source_target_pairs={{0,1},{1,2},{2,3},{3,0},{4,5},{5,6},{6,7},{7,4},{8,9},{9,10},{10,1... | collective-permute-start | bytes 1179656 | tf_op jit(solution)/shard_map/ppermute | solution.py:22
  155.5 12.5 %collective-permute-done.9 = bf16[128,1536]{1,0:T(8,128)(2,1)} collective-permute-done((bf16[128,1536]{1,0:T(8,128)(2,1)}, bf16[128,1536]{1,0:T(8,128)(2,1)}, u32[]{:S(2)}, u32[]{:S(2)}) %collective-permute-start.9) | collective-permute-done | bytes 393248 | tf_op jit(solution)/shard_map/ppermute | solution.py:22
  168.0 0.7 copy-done.15
  168.8 7.2 %fusion.136 = (f32[128]{0:T(128)S(1)}, f32[128,1536]{1,0:T(8,128)}) fusion(f32[128,1536]{1,0:T(8,128)} %copy-done.1, bf16[128,1536]{1,0:T(8,128)(2,1)} %collective-permute-done.11, bf16[128,1536]{1,0:T(8,128)(2,1)} %collective-permute-done.9, bf16[128,1536]{1,0:T(8,128)(2,1)} %copy-done.15, bf16[1536,1536]{1,0:T(8,128)(2,1)} %param.19, ...), kind=kOutput, calls=%fused_computation.185 | convolution fusion | flops 1212874624 | bytes 12209664 | tf_op jit(solution)/shard_map/dot_general | solution.py:132
  176.0 1.4 multiply_reduce_fusion
  177.4 1.5 fusion.137
  178.9 1.6 collective-permute-start.12
  182.7 0.6 multiply_reduce_fusion.2
  183.3 1.3 pad_maximum_fusion.3
  184.6 3.6 %collective-permute-done.13 = f32[2]{0:T(128)S(1)} collective-permute-done((f32[2]{0:T(128)S(1)}, f32[2]{0:T(128)S(1)}, u32[]{:S(2)}, u32[]{:S(2)}) %collective-permute-start.13) | collective-permute-done | bytes 40 | tf_op jit(solution)/shard_map/ppermute | solution.py:17
  188.1 1.3 fusion.167
  189.4 0.7 collective-permute-start.14
  190.1 3.8 %collective-permute-done.14 = f32[2]{0:T(128)S(1)} collective-permute-done((f32[2]{0:T(128)S(1)}, f32[2]{0:T(128)S(1)}, u32[]{:S(2)}, u32[]{:S(2)}) %collective-permute-start.14) | collective-permute-done | bytes 40 | tf_op jit(solution)/shard_map/ppermute | solution.py:17
  193.9 1.3 fusion.168
  195.2 0.6 fusion.134
  197.2 0.6 fusion.104
  (54 shorter events, 0.6 us)
Async XLA Ops:
  0.6 83.5 %copy-start = (bf16[1024,1536]{1,0:T(8,128)(2,1)S(1)}, bf16[1024,1536]{1,0:T(8,128)(2,1)}, u32[]{:S(2)}) copy-start(bf16[1024,1536]{1,0:T(8,128)(2,1)} %param.17) | copy-start | bytes 9437188
  10.3 20.6 %collective-permute-start.2 = (bf16[168,1536]{1,0:T(8,128)(2,1)}, bf16[168,1536]{1,0:T(8,128)(2,1)}, u32[]{:S(2)}, u32[]{:S(2)}) collective-permute-start(bf16[168,1536]{1,0:T(8,128)(2,1)} %get-tuple-element.35), channel_id=1, source_target_pairs={{0,1},{1,2},{2,3},{3,0},{4,5},{5,6},{6,7},{7,4},{8,9},{9,10},{10,1... | collective-permute-start | bytes 1548296 | tf_op jit(solution)/shard_map/ppermute | solution.py:22
  13.4 36.3 %collective-permute-start.1 = (bf16[168,1536]{1,0:T(8,128)(2,1)}, bf16[168,1536]{1,0:T(8,128)(2,1)}, u32[]{:S(2)}, u32[]{:S(2)}) collective-permute-start(bf16[168,1536]{1,0:T(8,128)(2,1)} %get-tuple-element.35), channel_id=1, source_target_pairs={{0,2},{1,3},{2,0},{3,1},{4,6},{5,7},{6,4},{7,5},{8,10},{9,11},{10,... | collective-permute-start | bytes 1548296 | tf_op jit(solution)/shard_map/ppermute | solution.py:22
  16.0 33.8 %collective-permute-start = (bf16[168,1536]{1,0:T(8,128)(2,1)}, bf16[168,1536]{1,0:T(8,128)(2,1)}, u32[]{:S(2)}, u32[]{:S(2)}) collective-permute-start(bf16[168,1536]{1,0:T(8,128)(2,1)} %get-tuple-element.35), channel_id=1, source_target_pairs={{0,3},{1,0},{2,1},{3,2},{4,7},{5,4},{6,5},{7,6},{8,11},{9,8},{10,9... | collective-permute-start | bytes 1548296 | tf_op jit(solution)/shard_map/ppermute | solution.py:22
  30.9 23.0 %copy-start.2 = (bf16[1536,4,2,64]{0,3,2,1:T(8,128)(2,1)S(1)}, bf16[1536,4,2,64]{0,3,2,1:T(8,128)(2,1)}, u32[]{:S(2)}) copy-start(bf16[1536,4,2,64]{0,3,2,1:T(8,128)(2,1)} %slice.117) | copy-start | bytes 4718596
  58.5 7.4 %copy-start.7 = (pred[672]{0:T(1024)(128)(4,1)S(1)}, pred[672]{0:T(1024)(128)(4,1)}, u32[]{:S(2)}) copy-start(pred[672]{0:T(1024)(128)(4,1)} %concatenate.12) | copy-start | bytes 2020
  65.9 3.5 %copy-start.4 = (bf16[160,4,64]{0,2,1:T(8,128)(2,1)S(1)}, bf16[160,4,64]{0,2,1:T(8,128)(2,1)}, u32[]{:S(2)}) copy-start(bf16[160,4,64]{0,2,1:T(8,128)(2,1)} %get-tuple-element.40) | copy-start | bytes 245764
  70.8 19.6 %copy-start.3 = (bf16[1,1,128,1536]{3,2,1,0:T(8,128)(2,1)S(1)}, bf16[1,1,128,1536]{3,2,1,0:T(8,128)(2,1)}, u32[]{:S(2)}) copy-start(bf16[1,1,128,1536]{3,2,1,0:T(8,128)(2,1)} %param.13) | copy-start | bytes 1179652
  70.8 19.5 %copy-start.5 = (f32[1536]{0:T(1024)S(1)}, f32[1536]{0:T(1024)}, u32[]{:S(2)}) copy-start(f32[1536]{0:T(1024)} %get-tuple-element.28) | copy-start | bytes 18436
  70.9 19.1 %collective-permute-start.5 = (bf16[128,256]{0,1:T(8,128)(2,1)S(1)}, bf16[128,256]{0,1:T(8,128)(2,1)S(1)}, u32[]{:S(2)}, u32[]{:S(2)}) collective-permute-start(bf16[128,256]{0,1:T(8,128)(2,1)S(1)} %bitcast.130), channel_id=1, source_target_pairs={{0,3},{1,0},{2,1},{3,2},{4,7},{5,4},{6,5},{7,6},{8,11},{9,8},{10,9... | collective-permute-start | bytes 196616 | tf_op jit(solution)/shard_map/ppermute | solution.py:22
  83.5 6.2 %collective-permute-start.3 = (bf16[128,256]{0,1:T(8,128)(2,1)S(1)}, bf16[128,256]{0,1:T(8,128)(2,1)S(1)}, u32[]{:S(2)}, u32[]{:S(2)}) collective-permute-start(bf16[128,256]{0,1:T(8,128)(2,1)S(1)} %bitcast.131), channel_id=1, source_target_pairs={{0,1},{1,2},{2,3},{3,0},{4,5},{5,6},{6,7},{7,4},{8,9},{9,10},{10,1... | collective-permute-start | bytes 196616 | tf_op jit(solution)/shard_map/ppermute | solution.py:22
  83.5 6.9 %collective-permute-start.4 = (bf16[128,256]{0,1:T(8,128)(2,1)S(1)}, bf16[128,256]{0,1:T(8,128)(2,1)S(1)}, u32[]{:S(2)}, u32[]{:S(2)}) collective-permute-start(bf16[128,256]{0,1:T(8,128)(2,1)S(1)} %bitcast.129), channel_id=1, source_target_pairs={{0,2},{1,3},{2,0},{3,1},{4,6},{5,7},{6,4},{7,5},{8,10},{9,11},{10,... | collective-permute-start | bytes 196616 | tf_op jit(solution)/shard_map/ppermute | solution.py:22
  90.8 0.9 copy-start.1
  90.8 5.1 %copy-start.11 = (f32[128]{0:T(128)}, f32[128]{0:T(128)S(1)}, u32[]{:S(2)}) copy-start(f32[128]{0:T(128)S(1)} %broadcast_multiply_fusion.2) | copy-start | bytes 1540
  91.0 4.9 %copy-start.13 = (f32[128]{0:T(128)}, f32[128]{0:T(128)S(1)}, u32[]{:S(2)}) copy-start(f32[128]{0:T(128)S(1)} %add_rsqrt_fusion.1) | copy-start | bytes 1540
  91.9 14.0 %collective-permute-start.10 = (bf16[128,1536]{1,0:T(8,128)(2,1)S(1)}, bf16[128,1536]{1,0:T(8,128)(2,1)}, u32[]{:S(2)}, u32[]{:S(2)}) collective-permute-start(bf16[128,1536]{1,0:T(8,128)(2,1)S(1)} %add_convert_fusion.1), channel_id=1, source_target_pairs={{0,1},{1,2},{2,3},{3,0},{4,5},{5,6},{6,7},{7,4},{8,9},{9,10},{10,1... | collective-permute-start | bytes 1179656 | tf_op jit(solution)/shard_map/ppermute | solution.py:22
  92.5 27.6 %collective-permute-start.8 = (bf16[128,1536]{1,0:T(8,128)(2,1)S(1)}, bf16[128,1536]{1,0:T(8,128)(2,1)}, u32[]{:S(2)}, u32[]{:S(2)}) collective-permute-start(bf16[128,1536]{1,0:T(8,128)(2,1)S(1)} %add_convert_fusion.1), channel_id=1, source_target_pairs={{0,2},{1,3},{2,0},{3,1},{4,6},{5,7},{6,4},{7,5},{8,10},{9,11},{10,... | collective-permute-start | bytes 1179656 | tf_op jit(solution)/shard_map/ppermute | solution.py:22
  94.6 52.6 %collective-permute-start.6 = (bf16[128,1536]{1,0:T(8,128)(2,1)S(1)}, bf16[128,1536]{1,0:T(8,128)(2,1)}, u32[]{:S(2)}, u32[]{:S(2)}) collective-permute-start(bf16[128,1536]{1,0:T(8,128)(2,1)S(1)} %add_convert_fusion.1), channel_id=1, source_target_pairs={{0,3},{1,0},{2,1},{3,2},{4,7},{5,4},{6,5},{7,6},{8,11},{9,8},{10,9... | collective-permute-start | bytes 1179656 | tf_op jit(solution)/shard_map/ppermute | solution.py:22
  112.2 43.3 %collective-permute-start.11 = (bf16[128,1536]{1,0:T(8,128)(2,1)}, bf16[128,1536]{1,0:T(8,128)(2,1)}, u32[]{:S(2)}, u32[]{:S(2)}) collective-permute-start(bf16[128,1536]{1,0:T(8,128)(2,1)} %convolution_convert_fusion), channel_id=1, source_target_pairs={{0,3},{1,0},{2,1},{3,2},{4,7},{5,4},{6,5},{7,6},{8,11},{9,8},{10,9... | collective-permute-start | bytes 1179656 | tf_op jit(solution)/shard_map/ppermute | solution.py:22
  126.3 41.7 %collective-permute-start.9 = (bf16[128,1536]{1,0:T(8,128)(2,1)}, bf16[128,1536]{1,0:T(8,128)(2,1)}, u32[]{:S(2)}, u32[]{:S(2)}) collective-permute-start(bf16[128,1536]{1,0:T(8,128)(2,1)} %convolution_convert_fusion.1), channel_id=1, source_target_pairs={{0,2},{1,3},{2,0},{3,1},{4,6},{5,7},{6,4},{7,5},{8,10},{9,11},{10,... | collective-permute-start | bytes 1179656 | tf_op jit(solution)/shard_map/ppermute | solution.py:22
  147.1 21.6 %copy-start.10 = (f32[1536]{0:T(1024)S(1)}, f32[1536]{0:T(1024)}, u32[]{:S(2)}) copy-start(f32[1536]{0:T(1024)} %get-tuple-element.17) | copy-start | bytes 18436
  147.1 21.6 %copy-start.12 = (f32[128]{0:T(128)S(1)}, f32[128]{0:T(128)}, u32[]{:S(2)}) copy-start(f32[128]{0:T(128)} %copy-done.11) | copy-start | bytes 1540
  147.1 21.6 %copy-start.14 = (f32[128]{0:T(128)S(1)}, f32[128]{0:T(128)}, u32[]{:S(2)}) copy-start(f32[128]{0:T(128)} %copy-done.13) | copy-start | bytes 1540
  153.5 14.5 %collective-permute-start.7 = (bf16[128,1536]{1,0:T(8,128)(2,1)}, bf16[128,1536]{1,0:T(8,128)(2,1)S(1)}, u32[]{:S(2)}, u32[]{:S(2)}) collective-permute-start(bf16[128,1536]{1,0:T(8,128)(2,1)} %convolution_convert_fusion.2), channel_id=1, source_target_pairs={{0,1},{1,2},{2,3},{3,0},{4,5},{5,6},{6,7},{7,4},{8,9},{9,10},{10,1... | collective-permute-start | bytes 1179656 | tf_op jit(solution)/shard_map/ppermute | solution.py:22
  168.0 0.7 copy-start.15
  168.7 8.6 %copy-start.8 = (f32[1536]{0:T(1024)S(1)}, f32[1536]{0:T(1024)}, u32[]{:S(2)}) copy-start(f32[1536]{0:T(1024)} %get-tuple-element.14) | copy-start | bytes 18436
  168.7 8.6 %copy-start.9 = (f32[1536]{0:T(1024)S(1)}, f32[1536]{0:T(1024)}, u32[]{:S(2)}) copy-start(f32[1536]{0:T(1024)} %get-tuple-element.29) | copy-start | bytes 18436
  168.7 8.6 %copy-start.16 = (bf16[64,1536]{1,0:T(8,128)(2,1)S(1)}, bf16[64,1536]{1,0:T(8,128)(2,1)}, u32[]{:S(2)}) copy-start(bf16[64,1536]{1,0:T(8,128)(2,1)} %param.20) | copy-start | bytes 589828
  168.8 28.4 %copy-start.6 = (f32[1,32,128]{2,1,0:T(8,128)S(1)}, f32[1,32,128]{2,1,0:T(8,128)}, u32[]{:S(2)}) copy-start(f32[1,32,128]{2,1,0:T(8,128)} %param.21) | copy-start | bytes 49156
  178.9 3.8 %collective-permute-start.12 = (bf16[64,128]{1,0:T(8,128)(2,1)S(1)}, bf16[64,128]{1,0:T(8,128)(2,1)S(1)}, u32[]{:S(2)}, u32[]{:S(2)}) collective-permute-start(bf16[64,128]{1,0:T(8,128)(2,1)S(1)} %get-tuple-element.53), channel_id=1, source_target_pairs={{0,16},{16,0},{1,17},{17,1},{2,18},{18,2},{3,19},{19,3},{4,20},{20... | collective-permute-start | bytes 49160 | tf_op jit(solution)/shard_map/ppermute | solution.py:17
  184.6 3.6 %collective-permute-start.13 = (f32[2]{0:T(128)S(1)}, f32[2]{0:T(128)S(1)}, u32[]{:S(2)}, u32[]{:S(2)}) collective-permute-start(f32[2]{0:T(128)S(1)} %pad_maximum_fusion.3), channel_id=1, source_target_pairs={{0,1},{1,0},{2,3},{3,2},{4,5},{5,4},{6,7},{7,6},{8,9},{9,8},{10,11... | collective-permute-start | bytes 32 | tf_op jit(solution)/shard_map/ppermute | solution.py:17
  189.4 4.5 %collective-permute-start.14 = (f32[2]{0:T(128)S(1)}, f32[2]{0:T(128)S(1)}, u32[]{:S(2)}, u32[]{:S(2)}) collective-permute-start(f32[2]{0:T(128)S(1)} %fusion.167), channel_id=1, source_target_pairs={{0,2},{1,3},{2,0},{3,1},{4,6},{5,7},{6,4},{7,5},{8,10},{9,11},{10,... | collective-permute-start | bytes 32 | tf_op jit(solution)/shard_map/ppermute | solution.py:17

commit v3 on v2

--- a/solution.py
+++ b/solution.py
@@ -70,9 +70,7 @@
     text_total = text_rows.shape[0] * seq_size
     image_norm = modulate(image_rows, mod_rows[1], mod_rows[0])
     text_norm = modulate(text_rows, mod_rows[4], mod_rows[3])
-    seq_index = lax.axis_index("seq")
-    own_norm = jnp.concatenate([image_norm, text_norm], axis=0)
-    gathered = jnp.stack([own_norm] + [shifted(own_norm, "seq", k) for k in range(1, seq_size)])
+    gathered = lax.all_gather(jnp.concatenate([image_norm, text_norm], axis=0), "seq", axis=0)
     image_all = gathered[:, :local_rows].reshape(image_total, -1)
     text_all = gathered[:, local_rows:].reshape(text_total, -1)
     image_cols, text_cols = split_columns(attn_weight)
@@ -86,9 +84,7 @@
     text_kv = text_kv.reshape(text_total, local_heads, 2, HEAD)
     keys_all = jnp.concatenate([image_qkv[:, :, 1], text_kv[:, :, 0]], axis=0)
     values_all = jnp.concatenate([image_qkv[:, :, 2], text_kv[:, :, 1]], axis=0)
-    text_local = text_rows.shape[0]
-    sources = (seq_index + jnp.arange(seq_size, dtype=jnp.int32)) % seq_size
-    slots = (sources[:, None] * text_local + jnp.arange(text_local, dtype=jnp.int32)).reshape(-1)
+    slots = jnp.arange(text_total, dtype=jnp.int32)
     valid = jnp.concatenate([jnp.ones((image_total,), dtype=bool), slots < text_lengths[0, 0]])
     block_rows = local_rows
     while block_rows < 512 and image_total % (block_rows * 2) == 0:
@@ -112,16 +108,10 @@
         return jnp.transpose(mixed.astype(jnp.bfloat16), (1, 0, 2))
 
     attended = lax.map(attend, query_blocks).reshape(image_total, local_heads * HEAD)
-    attended = attended.reshape(seq_size, local_rows, local_heads * HEAD)
-    head_width = local_heads * HEAD
-    projected = jnp.zeros((local_rows, proj_weight.shape[1]), jnp.float32)
-    for k in range(seq_size):
-        piece = attended[k] if k == 0 else shifted(attended[k], "seq", -k)
-        rows = lax.dynamic_slice_in_dim(
-            proj_weight, ((seq_index - k) % seq_size) * head_width, head_width, 0
-        )
-        projected = projected + jnp.dot(piece, rows, preferred_element_type=jnp.float32)
-    hidden = image_rows.astype(jnp.float32) + mod_rows[2] * projected
+    attended = lax.all_to_all(attended, "seq", split_axis=0, concat_axis=1, tiled=True)
+    hidden = image_rows.astype(jnp.float32) + mod_rows[2] * jnp.dot(
+        attended, proj_weight, preferred_element_type=jnp.float32
+    )
     mlp_norm = modulate(hidden, mod_rows[8], mod_rows[7])
     mlp_out = jnp.zeros((local_rows, mlp_out_weight.shape[1]), jnp.float32)
     for k in range(seq_size):

time: 199 us -> 214 us (1.075)
  starting transfers between devices: 50.2 us -> 31.2 us
  between operations: 5 us -> 18.3 us
  blocking collectives: 0 us -> 11.5 us
  waiting for transfers between devices: 61.2 us -> 67.2 us
  local copies, waits for them, and re-layouts: 21.5 us -> 26.5 us
  other arithmetic: 22 us -> 17.5 us
  matrix products: 37.9 us -> 40.6 us
    all_gather x0 -> x1, waiting for transfers between devices: none -> 34.3 us  [local(): lax.all_gather(jnp.concatenate([image_norm, text_norm], axis=0), 'seq', a...]
    ppermute x12 -> x6, waiting for transfers between devices: 53.7 us -> 28.4 us  [shifted(): lax.ppermute(value, axis, [(source, (source - shift) % size) for source i...]
    ppermute x12 -> x6, starting transfers between devices: 47.9 us -> 25.8 us  [shifted(): lax.ppermute(value, axis, [(source, (source - shift) % size) for source i...]
    all_to_all x0 -> x1, blocking collectives: none -> 11.5 us  [local(): lax.all_to_all(attended, 'seq', split_axis=0, concat_axis=1, tiled=True)]
    another operation x2 -> x0, other arithmetic: 4.14 us -> none  [local(): jnp.stack([own_norm] + [shifted(own_norm, 'seq', k) for k in range(1, seq...]
    ppermute x3, starting transfers between devices: 2.31 us -> 5.36 us  [partner(): return lax.ppermute(value, axis, pairs)]
    ppermute x3, waiting for transfers between devices: 7.49 us -> 4.45 us  [partner(): return lax.ppermute(value, axis, pairs)]
    all_to_all x0 -> x2, local copies, waits for them, and re-layouts: none -> 2.7 us  [local(): lax.all_to_all(attended, 'seq', split_axis=0, concat_axis=1, tiled=True)]
  transfers between devices with their start and end apart: 15 -> 10, of which waited for: 9 -> 7; matrix products, arithmetic and copies ran while one was open for 17% -> 15% of each run, Pallas kernels for 0% -> 0%
where the time goes in v3:
time: 214 us; the launch traced here: 213 us
  waiting for transfers between devices  67.2 us (31%)
  matrix products  40.6 us (19%)
  starting transfers between devices  31.2 us (15%)
  local copies, waits for them, and re-layouts  26.5 us (12%)
  between operations  18.3 us (9%)
  other arithmetic  17.5 us (8%)
  blocking collectives  11.5 us (5%)
    all_gather x1, waiting for transfers between devices, local(): lax.all_gather(jnp.concatenate([image_norm, text_norm], axis=0), 'seq', a...  34.3 us
    ppermute x6, waiting for transfers between devices, shifted(): lax.ppermute(value, axis, [(source, (source - shift) % size) for source i...  28.4 us
    dot_general x4, matrix products, local(): jnp.dot(inner, mlp_out_weight, preferred_element_type=jnp.float32)  26.1 us
    ppermute x6, starting transfers between devices, shifted(): lax.ppermute(value, axis, [(source, (source - shift) % size) for source i...  25.8 us
    all_to_all x1, blocking collectives, local(): lax.all_to_all(attended, 'seq', split_axis=0, concat_axis=1, tiled=True)  11.5 us
    unnamed x33, local copies, waits for them, and re-layouts  7.7 us
    ppermute x3, starting transfers between devices, partner(): return lax.ppermute(value, axis, pairs)  5.36 us
    dot_general x1, matrix products, local(): jnp.dot(image_all, image_cols, preferred_element_type=jnp.float32)  4.45 us
  transfers between devices with their start and end apart: 10, of which 7 were waited for; matrix products, arithmetic and copies ran while one was open for 15% of the time, Pallas kernels for 0%

profile of v3, /device:TPU:0, one launch (start us, length us, event | category | flops | bytes accessed | tf_op | source)
XLA Modules:
  0.0 212.8 jit_solution(5999286143037610245)
XLA Ops:
  7.2 0.0 copy-start
  7.2 0.0 all-gather.3.cloned.1.call-start
  7.2 1.7 add_reduce_fusion
  9.0 1.0 convert_reduce_fusion.1
  10.0 1.1 fusion.92
  11.1 1.1 convert_reduce_fusion
  12.3 1.2 fusion.20
  13.5 1.0 fusion.95
  14.5 1.3 fusion.23
  15.8 0.8 pad_maximum_fusion
  16.7 0.0 all-gather.3.cloned.1.call-update
  16.7 6.3 %copy.20 = bf16[1536,1280]{0,1:T(8,128)(2,1)} copy(bf16[1536,1280]{1,0:T(8,128)(2,1)} %param.16) | data formatting | bytes 7864320 | tf_op args[3]
  23.0 2.8 %slice.98 = bf16[1536,4,2,64]{0,3,2,1:T(8,128)(2,1)} slice(bf16[1536,4,5,64]{0,3,2,1:T(8,128)(2,1)} %bitcast.114), slice={[0:1536], [0:4], [3:5], [0:64]} | slice | bytes 3145728 | tf_op jit(solution)/shard_map/slice | solution.py:44
  25.7 3.4 %slice.95 = bf16[1536,4,3,64]{0,3,2,1:T(8,128)(2,1)} slice(bf16[1536,4,5,64]{0,3,2,1:T(8,128)(2,1)} %bitcast.115), slice={[0:1536], [0:4], [0:3], [0:64]} | slice | bytes 4718592 | tf_op jit(solution)/shard_map/slice | solution.py:43
  29.8 0.6 concatenate.12
  30.4 34.3 %all-gather.3.cloned.1.call-done = bf16[672,1536]{1,0:T(8,128)(2,1)} async-done(((bf16[168,1536]{1,0:T(8,128)(2,1)}), bf16[672,1536]{1,0:T(8,128)(2,1)}) %all-gather.3.cloned.1.call-update) | async-done | bytes 2064400 | tf_op jit(solution)/shard_map/all_gather | solution.py:73
  64.7 1.1 slice.97
  65.8 2.7 %slice.94 = bf16[4,128,1536]{2,1,0:T(8,128)(2,1)} slice(bf16[4,168,1536]{2,1,0:T(8,128)(2,1)} %bitcast.121), slice={[0:4], [0:128], [0:1536]} | slice | bytes 3145728 | tf_op jit(solution)/shard_map/slice | solution.py:74
  68.4 2.7 %convolution_convert_fusion.5 = bf16[160,512]{1,0:T(8,128)(2,1)} fusion(bf16[160,1536]{1,0:T(8,128)(2,1)S(1)} %bitcast.122, bf16[1536,512]{0,1:T(8,128)(2,1)} %bitcast.116), kind=kOutput, calls=%fused_computation.20 | convolution fusion | flops 251740160 | bytes 2228224 | tf_op jit(solution)/shard_map/dot_general | solution.py:80
  71.2 1.0 copy.24
  72.2 0.7 slice_bitcast_fusion.5
  72.9 4.5 %convolution_convert_fusion.4 = bf16[512,768]{1,0:T(8,128)(2,1)} fusion(bf16[512,1536]{1,0:T(8,128)(2,1)} %bitcast.123, bf16[1536,768]{0,1:T(8,128)(2,1)} %bitcast.119), kind=kOutput, calls=%fused_computation.14 | convolution fusion | flops 1208352768 | bytes 4718592 | tf_op jit(solution)/shard_map/dot_general | solution.py:77
  77.3 2.3 %copy.21 = bf16[512,768]{0,1:T(8,128)(2,1)} copy(bf16[512,768]{1,0:T(8,128)(2,1)} %convolution_convert_fusion.4) | data formatting | bytes 1572864 | tf_op jit(solution)/shard_map/convert_element_type | solution.py:77
  79.6 1.1 slice_bitcast_fusion.3
  80.7 2.4 %fusion = (f32[4,512]{1,0:T(4,128)S(1)}, f32[4,512,672]{1,2,0:T(8,128)S(1)}) fusion(pred[672]{0:T(1024)(128)(4,1)S(1)} %copy-done.5, bf16[160,4,64]{0,2,1:T(8,128)(2,1)S(1)} %get-tuple-element.35, bf16[512,4,64]{0,2,1:T(8,128)(2,1)S(1)} %get-tuple-element.33, bf16[512,4,3,64]{0,3,2,1:T(8,128)(2,1)} %bitcast.118), kind=kOutput, calls=%fused_computation.2 | convolution fusion | flops 180975616 | bytes 6120096 | tf_op jit(solution)/shard_map/while/body/eval_jaxpr/qhe,khe->hqk/dot_general | solution.py:96
  83.1 1.2 fusion.1
  84.3 0.0 copy-start.2
  84.3 2.1 fusion.14
  86.3 1.7 all_to_all.14
  88.1 1.0 copy.28
  89.0 11.5 %all_to_all.19 = bf16[4,128,256]{1,2,0:T(8,128)(2,1)S(1)} all-to-all(bf16[4,128,256]{1,2,0:T(8,128)(2,1)S(1)} %copy.28), channel_id=1, replica_groups=mesh['cfg'=2,'req'=4,'seq'=4] {'seq'}, dimensions={0} | all-to-all | bytes 524288 | tf_op jit(solution)/shard_map/all_to_all | solution.py:111
  100.6 1.4 fusion.119
  102.0 0.2 multiply_reduce_fusion.1
  102.2 0.6 copy-done.1
  102.8 0.2 add_convert_fusion.1
  103.0 0.3 collective-permute-start.4
  103.3 1.8 collective-permute-start.2
  105.1 1.8 collective-permute-start
  106.9 10.2 %collective-permute-done.4 = bf16[128,1536]{1,0:T(8,128)(2,1)} collective-permute-done((bf16[128,1536]{1,0:T(8,128)(2,1)S(1)}, bf16[128,1536]{1,0:T(8,128)(2,1)}, u32[]{:S(2)}, u32[]{:S(2)}) %collective-permute-start.4) | collective-permute-done | bytes 393248 | tf_op jit(solution)/shard_map/ppermute | solution.py:22
  117.1 6.3 %convolution_convert_fusion = bf16[128,1536]{1,0:T(8,128)(2,1)} fusion(bf16[1536,1536]{1,0:T(8,128)(2,1)} %param.19, bf16[128,1536]{1,0:T(8,128)(2,1)} %collective-permute-done.4, bf16[1536,1536]{1,0:T(8,128)(2,1)} %param.18), kind=kOutput, calls=%fused_computation.9 | convolution fusion | flops 1209925632 | bytes 10223616 | tf_op jit(solution)/shard_map/dot_general | solution.py:122
  123.4 7.4 %collective-permute-done.2 = bf16[128,1536]{1,0:T(8,128)(2,1)} collective-permute-done((bf16[128,1536]{1,0:T(8,128)(2,1)S(1)}, bf16[128,1536]{1,0:T(8,128)(2,1)}, u32[]{:S(2)}, u32[]{:S(2)}) %collective-permute-start.2) | collective-permute-done | bytes 393248 | tf_op jit(solution)/shard_map/ppermute | solution.py:22
  130.8 6.3 %convolution_convert_fusion.1 = bf16[128,1536]{1,0:T(8,128)(2,1)} fusion(bf16[1536,1536]{1,0:T(8,128)(2,1)} %param.19, bf16[128,1536]{1,0:T(8,128)(2,1)} %collective-permute-done.2, bf16[1536,1536]{1,0:T(8,128)(2,1)} %param.18), kind=kOutput, calls=%fused_computation.10 | convolution fusion | flops 1209925632 | bytes 10223616 | tf_op jit(solution)/shard_map/dot_general | solution.py:122
  137.1 16.2 %collective-permute-start.3 = (bf16[128,1536]{1,0:T(8,128)(2,1)}, bf16[128,1536]{1,0:T(8,128)(2,1)}, u32[]{:S(2)}, u32[]{:S(2)}) collective-permute-start(bf16[128,1536]{1,0:T(8,128)(2,1)} %convolution_convert_fusion.1), channel_id=1, source_target_pairs={{0,2},{1,3},{2,0},{3,1},{4,6},{5,7},{6,4},{7,5},{8,10},{9,11},{10,... | collective-permute-start | bytes 1179656 | tf_op jit(solution)/shard_map/ppermute | solution.py:22
  153.3 6.3 %convolution_convert_fusion.2 = bf16[128,1536]{1,0:T(8,128)(2,1)} fusion(bf16[1536,1536]{1,0:T(8,128)(2,1)} %param.19, bf16[128,1536]{1,0:T(8,128)(2,1)} %collective-permute-done, bf16[1536,1536]{1,0:T(8,128)(2,1)} %param.18), kind=kOutput, calls=%fused_computation.11 | convolution fusion | flops 1209925632 | bytes 10223616 | tf_op jit(solution)/shard_map/dot_general | solution.py:122
  159.6 5.8 %collective-permute-start.1 = (bf16[128,1536]{1,0:T(8,128)(2,1)}, bf16[128,1536]{1,0:T(8,128)(2,1)S(1)}, u32[]{:S(2)}, u32[]{:S(2)}) collective-permute-start(bf16[128,1536]{1,0:T(8,128)(2,1)} %convolution_convert_fusion.2), channel_id=1, source_target_pairs={{0,1},{1,2},{2,3},{3,0},{4,5},{5,6},{6,7},{7,4},{8,9},{9,10},{10,1... | collective-permute-start | bytes 1179656 | tf_op jit(solution)/shard_map/ppermute | solution.py:22
  165.4 10.8 %collective-permute-done.3 = bf16[128,1536]{1,0:T(8,128)(2,1)} collective-permute-done((bf16[128,1536]{1,0:T(8,128)(2,1)}, bf16[128,1536]{1,0:T(8,128)(2,1)}, u32[]{:S(2)}, u32[]{:S(2)}) %collective-permute-start.3) | collective-permute-done | bytes 393248 | tf_op jit(solution)/shard_map/ppermute | solution.py:22
  176.2 0.7 copy-done.14
  176.9 0.0 copy-start.15
  177.0 0.0 copy-start.4
  177.0 7.2 %fusion.120 = (f32[128]{0:T(128)S(1)}, f32[128,1536]{1,0:T(8,128)}) fusion(f32[128,1536]{1,0:T(8,128)} %copy-done.1, bf16[128,1536]{1,0:T(8,128)(2,1)} %collective-permute-done.5, bf16[128,1536]{1,0:T(8,128)(2,1)} %collective-permute-done.3, bf16[128,1536]{1,0:T(8,128)(2,1)} %copy-done.14, bf16[1536,1536]{1,0:T(8,128)(2,1)} %param.19, ...), kind=kOutput, calls=%fused_computation.163 | convolution fusion | flops 1212874624 | bytes 12209664 | tf_op jit(solution)/shard_map/dot_general | solution.py:122
  184.2 1.4 multiply_reduce_fusion
  185.6 1.5 fusion.121
  187.1 1.4 collective-permute-start.6
  190.5 0.3 collective-permute-done.6
  190.9 0.6 multiply_reduce_fusion.2
  191.5 1.3 pad_maximum_fusion.1
  192.8 1.1 collective-permute-start.7
  193.8 2.5 %collective-permute-done.7 = f32[2]{0:T(128)S(1)} collective-permute-done((f32[2]{0:T(128)S(1)}, f32[2]{0:T(128)S(1)}, u32[]{:S(2)}, u32[]{:S(2)}) %collective-permute-start.7) | collective-permute-done | bytes 40 | tf_op jit(solution)/shard_map/ppermute | solution.py:17
  196.3 1.3 fusion.149
  197.6 2.9 %collective-permute-start.8 = (f32[2]{0:T(128)S(1)}, f32[2]{0:T(128)S(1)}, u32[]{:S(2)}, u32[]{:S(2)}) collective-permute-start(f32[2]{0:T(128)S(1)} %fusion.149), channel_id=1, source_target_pairs={{0,2},{1,3},{2,0},{3,1},{4,6},{5,7},{6,4},{7,5},{8,10},{9,11},{10,... | collective-permute-start | bytes 32 | tf_op jit(solution)/shard_map/ppermute | solution.py:17
  200.5 1.6 collective-permute-done.8
  202.1 1.3 fusion.150
  203.4 0.6 fusion.118
  205.3 0.6 fusion.96
  (39 shorter events, 0.1 us)
Async XLA Ops:
  7.2 93.4 %copy-start = (bf16[1024,1536]{1,0:T(8,128)(2,1)S(1)}, bf16[1024,1536]{1,0:T(8,128)(2,1)}, u32[]{:S(2)}) copy-start(bf16[1024,1536]{1,0:T(8,128)(2,1)} %param.17) | copy-start | bytes 9437188
  7.2 57.5 %all-gather.3.cloned.1.call-start = ((), (), s32[]{:S(2)}) async-start(), calls=%async_computation.1 | async-start | bytes 2580480 | tf_op jit(solution)/shard_map/all_gather | solution.py:73
  72.9 7.8 %copy-start.5 = (pred[672]{0:T(1024)(128)(4,1)S(1)}, pred[672]{0:T(1024)(128)(4,1)}, u32[]{:S(2)}) copy-start(pred[672]{0:T(1024)(128)(4,1)} %concatenate.12) | copy-start | bytes 2020
  80.7 3.6 %copy-start.3 = (bf16[160,4,64]{0,2,1:T(8,128)(2,1)S(1)}, bf16[160,4,64]{0,2,1:T(8,128)(2,1)}, u32[]{:S(2)}) copy-start(bf16[160,4,64]{0,2,1:T(8,128)(2,1)} %get-tuple-element.34) | copy-start | bytes 245764
  80.7 3.6 %copy-start.6 = (pred[672]{0:T(1024)(128)(4,1)S(1)}, pred[672]{0:T(1024)(128)(4,1)}, u32[]{:S(2)}) copy-start(pred[672]{0:T(1024)(128)(4,1)} %concatenate.12) | copy-start | bytes 2020
  84.3 16.3 %copy-start.2 = (bf16[1,1,128,1536]{3,2,1,0:T(8,128)(2,1)S(1)}, bf16[1,1,128,1536]{3,2,1,0:T(8,128)(2,1)}, u32[]{:S(2)}) copy-start(bf16[1,1,128,1536]{3,2,1,0:T(8,128)(2,1)} %param.13) | copy-start | bytes 1179652
  101.9 0.9 copy-start.1
  102.0 4.9 %copy-start.10 = (f32[128]{0:T(128)}, f32[128]{0:T(128)S(1)}, u32[]{:S(2)}) copy-start(f32[128]{0:T(128)S(1)} %broadcast_multiply_fusion.2) | copy-start | bytes 1540
  102.2 4.7 %copy-start.12 = (f32[128]{0:T(128)}, f32[128]{0:T(128)S(1)}, u32[]{:S(2)}) copy-start(f32[128]{0:T(128)S(1)} %add_rsqrt_fusion.1) | copy-start | bytes 1540
  103.0 14.0 %collective-permute-start.4 = (bf16[128,1536]{1,0:T(8,128)(2,1)S(1)}, bf16[128,1536]{1,0:T(8,128)(2,1)}, u32[]{:S(2)}, u32[]{:S(2)}) collective-permute-start(bf16[128,1536]{1,0:T(8,128)(2,1)S(1)} %add_convert_fusion.1), channel_id=1, source_target_pairs={{0,1},{1,2},{2,3},{3,0},{4,5},{5,6},{6,7},{7,4},{8,9},{9,10},{10,1... | collective-permute-start | bytes 1179656 | tf_op jit(solution)/shard_map/ppermute | solution.py:22
  103.3 27.5 %collective-permute-start.2 = (bf16[128,1536]{1,0:T(8,128)(2,1)S(1)}, bf16[128,1536]{1,0:T(8,128)(2,1)}, u32[]{:S(2)}, u32[]{:S(2)}) collective-permute-start(bf16[128,1536]{1,0:T(8,128)(2,1)S(1)} %add_convert_fusion.1), channel_id=1, source_target_pairs={{0,2},{1,3},{2,0},{3,1},{4,6},{5,7},{6,4},{7,5},{8,10},{9,11},{10,... | collective-permute-start | bytes 1179656 | tf_op jit(solution)/shard_map/ppermute | solution.py:22
  105.1 48.1 %collective-permute-start = (bf16[128,1536]{1,0:T(8,128)(2,1)S(1)}, bf16[128,1536]{1,0:T(8,128)(2,1)}, u32[]{:S(2)}, u32[]{:S(2)}) collective-permute-start(bf16[128,1536]{1,0:T(8,128)(2,1)S(1)} %add_convert_fusion.1), channel_id=1, source_target_pairs={{0,3},{1,0},{2,1},{3,2},{4,7},{5,4},{6,5},{7,6},{8,11},{9,8},{10,9... | collective-permute-start | bytes 1179656 | tf_op jit(solution)/shard_map/ppermute | solution.py:22
  123.4 42.0 %collective-permute-start.5 = (bf16[128,1536]{1,0:T(8,128)(2,1)}, bf16[128,1536]{1,0:T(8,128)(2,1)}, u32[]{:S(2)}, u32[]{:S(2)}) collective-permute-start(bf16[128,1536]{1,0:T(8,128)(2,1)} %convolution_convert_fusion), channel_id=1, source_target_pairs={{0,3},{1,0},{2,1},{3,2},{4,7},{5,4},{6,5},{7,6},{8,11},{9,8},{10,9... | collective-permute-start | bytes 1179656 | tf_op jit(solution)/shard_map/ppermute | solution.py:22
  137.1 39.1 %collective-permute-start.3 = (bf16[128,1536]{1,0:T(8,128)(2,1)}, bf16[128,1536]{1,0:T(8,128)(2,1)}, u32[]{:S(2)}, u32[]{:S(2)}) collective-permute-start(bf16[128,1536]{1,0:T(8,128)(2,1)} %convolution_convert_fusion.1), channel_id=1, source_target_pairs={{0,2},{1,3},{2,0},{3,1},{4,6},{5,7},{6,4},{7,5},{8,10},{9,11},{10,... | collective-permute-start | bytes 1179656 | tf_op jit(solution)/shard_map/ppermute | solution.py:22
  153.3 23.7 %copy-start.9 = (f32[1536]{0:T(1024)S(1)}, f32[1536]{0:T(1024)}, u32[]{:S(2)}) copy-start(f32[1536]{0:T(1024)} %get-tuple-element.17) | copy-start | bytes 18436
  153.3 23.7 %copy-start.11 = (f32[128]{0:T(128)S(1)}, f32[128]{0:T(128)}, u32[]{:S(2)}) copy-start(f32[128]{0:T(128)} %copy-done.10) | copy-start | bytes 1540
  153.3 23.7 %copy-start.13 = (f32[128]{0:T(128)S(1)}, f32[128]{0:T(128)}, u32[]{:S(2)}) copy-start(f32[128]{0:T(128)} %copy-done.12) | copy-start | bytes 1540
  159.6 16.6 %collective-permute-start.1 = (bf16[128,1536]{1,0:T(8,128)(2,1)}, bf16[128,1536]{1,0:T(8,128)(2,1)S(1)}, u32[]{:S(2)}, u32[]{:S(2)}) collective-permute-start(bf16[128,1536]{1,0:T(8,128)(2,1)} %convolution_convert_fusion.2), channel_id=1, source_target_pairs={{0,1},{1,2},{2,3},{3,0},{4,5},{5,6},{6,7},{7,4},{8,9},{9,10},{10,1... | collective-permute-start | bytes 1179656 | tf_op jit(solution)/shard_map/ppermute | solution.py:22
  176.2 0.7 copy-start.14
  176.9 8.6 %copy-start.7 = (f32[1536]{0:T(1024)S(1)}, f32[1536]{0:T(1024)}, u32[]{:S(2)}) copy-start(f32[1536]{0:T(1024)} %get-tuple-element.14) | copy-start | bytes 18436
  176.9 8.6 %copy-start.8 = (f32[1536]{0:T(1024)S(1)}, f32[1536]{0:T(1024)}, u32[]{:S(2)}) copy-start(f32[1536]{0:T(1024)} %get-tuple-element.29) | copy-start | bytes 18436
  176.9 8.6 %copy-start.15 = (bf16[64,1536]{1,0:T(8,128)(2,1)S(1)}, bf16[64,1536]{1,0:T(8,128)(2,1)}, u32[]{:S(2)}) copy-start(bf16[64,1536]{1,0:T(8,128)(2,1)} %param.20) | copy-start | bytes 589828
  177.0 28.4 %copy-start.4 = (f32[1,32,128]{2,1,0:T(8,128)S(1)}, f32[1,32,128]{2,1,0:T(8,128)}, u32[]{:S(2)}) copy-start(f32[1,32,128]{2,1,0:T(8,128)} %param.21) | copy-start | bytes 49156
  187.1 3.8 %collective-permute-start.6 = (bf16[64,128]{1,0:T(8,128)(2,1)S(1)}, bf16[64,128]{1,0:T(8,128)(2,1)S(1)}, u32[]{:S(2)}, u32[]{:S(2)}) collective-permute-start(bf16[64,128]{1,0:T(8,128)(2,1)S(1)} %get-tuple-element.47), channel_id=1, source_target_pairs={{0,16},{16,0},{1,17},{17,1},{2,18},{18,2},{3,19},{19,3},{4,20},{20... | collective-permute-start | bytes 49160 | tf_op jit(solution)/shard_map/ppermute | solution.py:17
  192.8 3.6 %collective-permute-start.7 = (f32[2]{0:T(128)S(1)}, f32[2]{0:T(128)S(1)}, u32[]{:S(2)}, u32[]{:S(2)}) collective-permute-start(f32[2]{0:T(128)S(1)} %pad_maximum_fusion.1), channel_id=1, source_target_pairs={{0,1},{1,0},{2,3},{3,2},{4,5},{5,4},{6,7},{7,6},{8,9},{9,8},{10,11... | collective-permute-start | bytes 32 | tf_op jit(solution)/shard_map/ppermute | solution.py:17
  197.6 4.5 %collective-permute-start.8 = (f32[2]{0:T(128)S(1)}, f32[2]{0:T(128)S(1)}, u32[]{:S(2)}, u32[]{:S(2)}) collective-permute-start(f32[2]{0:T(128)S(1)} %fusion.149), channel_id=1, source_target_pairs={{0,2},{1,3},{2,0},{3,1},{4,6},{5,7},{6,4},{7,5},{8,10},{9,11},{10,... | collective-permute-start | bytes 32 | tf_op jit(solution)/shard_map/ppermute | solution.py:17
Sparse Core Ops, SparseCore 0:
  16.8 47.8 all-gather.2

commit v4 on v2

--- a/solution.py
+++ b/solution.py
@@ -72,16 +72,23 @@
     text_norm = modulate(text_rows, mod_rows[4], mod_rows[3])
     seq_index = lax.axis_index("seq")
     own_norm = jnp.concatenate([image_norm, text_norm], axis=0)
-    gathered = jnp.stack([own_norm] + [shifted(own_norm, "seq", k) for k in range(1, seq_size)])
-    image_all = gathered[:, :local_rows].reshape(image_total, -1)
-    text_all = gathered[:, local_rows:].reshape(text_total, -1)
     image_cols, text_cols = split_columns(attn_weight)
-    image_qkv = jnp.dot(image_all, image_cols, preferred_element_type=jnp.float32).astype(
-        jnp.bfloat16
-    )
-    text_kv = jnp.dot(text_all, text_cols, preferred_element_type=jnp.float32).astype(
-        jnp.bfloat16
-    )
+    image_parts = []
+    text_parts = []
+    for k in range(seq_size):
+        piece = own_norm if k == 0 else shifted(own_norm, "seq", k)
+        image_parts.append(
+            jnp.dot(piece[:local_rows], image_cols, preferred_element_type=jnp.float32).astype(
+                jnp.bfloat16
+            )
+        )
+        text_parts.append(
+            jnp.dot(piece[local_rows:], text_cols, preferred_element_type=jnp.float32).astype(
+                jnp.bfloat16
+            )
+        )
+    image_qkv = jnp.concatenate(image_parts, axis=0)
+    text_kv = jnp.concatenate(text_parts, axis=0)
     image_qkv = image_qkv.reshape(image_total, local_heads, 3, HEAD)
     text_kv = text_kv.reshape(text_total, local_heads, 2, HEAD)
     keys_all = jnp.concatenate([image_qkv[:, :, 1], text_kv[:, :, 0]], axis=0)

time: 199 us -> 200 us (level)
  matrix products: 37.9 us -> 49.7 us
  waiting for transfers between devices: 61.2 us -> 51.2 us
  local copies, waits for them, and re-layouts: 21.5 us -> 23.7 us
    dot_general x2 -> x8, matrix products: 5.3 us -> 17.1 us  [the longest x4 10.6 us: local(): jnp.dot(piece[:local_rows], image_cols, preferred_element_type=jnp.float32)]
    ppermute x12, waiting for transfers between devices: 53.7 us -> 43.5 us  [shifted(): lax.ppermute(value, axis, [(source, (source - shift) % size) for source i...]
    another operation x2 -> x0, other arithmetic: 4.14 us -> none  [local(): jnp.stack([own_norm] + [shifted(own_norm, 'seq', k) for k in range(1, seq...]
    concatenate x0 -> x2, local copies, waits for them, and re-layouts: none -> 4.05 us  [the longest x1 2.29 us: local(): image_qkv = jnp.concatenate(image_parts, axis=0)]
    convert_element_type x2 -> x0, local copies, waits for them, and re-layouts: 3.36 us -> none  [the longest x1 2.32 us: local(): jnp.dot(image_all, image_cols, preferred_element_type=jnp.float32)]
    concatenate x0 -> x3, other arithmetic: none -> 2.46 us  [the longest x1 0.96 us: local(): image_qkv = jnp.concatenate(image_parts, axis=0)]
    unnamed x35 -> x55, local copies, waits for them, and re-layouts: 7.69 us -> 7.73 us
  transfers between devices with their start and end apart: 15 -> 15, of which waited for: 9 -> 8; matrix products, arithmetic and copies ran while one was open for 17% -> 22% of each run, Pallas kernels for 0% -> 0%
where the time goes in v4:
time: 200 us; the launch traced here: 199 us
  waiting for transfers between devices  51.2 us (26%)
  matrix products  49.7 us (25%)
  starting transfers between devices  48.7 us (24%)
  local copies, waits for them, and re-layouts  23.7 us (12%)
  other arithmetic  21 us (10%)
  between operations  5.16 us (3%)
    ppermute x12, starting transfers between devices, shifted(): lax.ppermute(value, axis, [(source, (source - shift) % size) for source i...  46.6 us
    ppermute x12, waiting for transfers between devices, shifted(): lax.ppermute(value, axis, [(source, (source - shift) % size) for source i...  43.5 us
    dot_general x4, matrix products, local(): jnp.dot(inner, mlp_out_weight, preferred_element_type=jnp.float32)  26.1 us
    dot_general x4, matrix products, local(): jnp.dot(piece[:local_rows], image_cols, preferred_element_type=jnp.float32)  10.6 us
    unnamed x55, local copies, waits for them, and re-layouts  7.73 us
    ppermute x3, waiting for transfers between devices, partner(): return lax.ppermute(value, axis, pairs)  7.72 us
    dot_general x4, matrix products, local(): jnp.dot(piece[local_rows:], text_cols, preferred_element_type=jnp.float32)  6.5 us
  transfers between devices with their start and end apart: 15, of which 8 were waited for; matrix products, arithmetic and copies ran while one was open for 22% of the time, Pallas kernels for 0%

profile of v4, /device:TPU:0, one launch (start us, length us, event | category | flops | bytes accessed | tf_op | source)
XLA Modules:
  0.0 199.4 jit_solution(3749987773879183581)
XLA Ops:
  0.6 1.7 add_reduce_fusion
  2.4 1.0 convert_reduce_fusion.1
  3.4 1.1 fusion.113
  4.6 1.1 convert_reduce_fusion
  5.7 1.2 fusion.22
  7.0 1.0 fusion.116
  8.1 1.3 fusion.25
  9.4 0.8 pad_maximum_fusion.1
  10.2 3.1 %collective-permute-start.2 = (bf16[168,1536]{1,0:T(8,128)(2,1)}, bf16[168,1536]{1,0:T(8,128)(2,1)}, u32[]{:S(2)}, u32[]{:S(2)}) collective-permute-start(bf16[168,1536]{1,0:T(8,128)(2,1)} %pad_maximum_fusion.1), channel_id=1, source_target_pairs={{0,1},{1,2},{2,3},{3,0},{4,5},{5,6},{6,7},{7,4},{8,9},{9,10},{10,1... | collective-permute-start | bytes 1548296 | tf_op jit(solution)/shard_map/ppermute | solution.py:22
  13.2 2.6 %collective-permute-start.1 = (bf16[168,1536]{1,0:T(8,128)(2,1)}, bf16[168,1536]{1,0:T(8,128)(2,1)}, u32[]{:S(2)}, u32[]{:S(2)}) collective-permute-start(bf16[168,1536]{1,0:T(8,128)(2,1)} %pad_maximum_fusion.1), channel_id=1, source_target_pairs={{0,2},{1,3},{2,0},{3,1},{4,6},{5,7},{6,4},{7,5},{8,10},{9,11},{10,... | collective-permute-start | bytes 1548296 | tf_op jit(solution)/shard_map/ppermute | solution.py:22
  15.8 1.3 collective-permute-start
  17.2 6.3 %copy.20 = bf16[1536,1280]{0,1:T(8,128)(2,1)} copy(bf16[1536,1280]{1,0:T(8,128)(2,1)} %param.16) | data formatting | bytes 7864320 | tf_op args[3]
  23.5 2.7 %slice.135 = bf16[1536,4,2,64]{0,3,2,1:T(8,128)(2,1)} slice(bf16[1536,4,5,64]{0,3,2,1:T(8,128)(2,1)} %bitcast.130), slice={[0:1536], [0:4], [3:5], [0:64]} | slice | bytes 3145728 | tf_op jit(solution)/shard_map/slice | solution.py:44
  26.2 3.2 %slice.130 = bf16[1536,4,3,64]{0,3,2,1:T(8,128)(2,1)} slice(bf16[1536,4,5,64]{0,3,2,1:T(8,128)(2,1)} %bitcast.131), slice={[0:1536], [0:4], [0:3], [0:64]} | slice | bytes 4718592 | tf_op jit(solution)/shard_map/slice | solution.py:43
  29.4 0.5 fusion.136
  30.6 1.3 add_compare_fusion
  31.9 1.3 lt.52
  33.1 1.2 concatenate.18
  34.3 3.4 %convolution_convert_fusion.7 = bf16[128,768]{1,0:T(8,128)(2,1)} fusion(bf16[1536,768]{0,1:T(8,128)(2,1)} %bitcast.126, bf16[1,1,128,1536]{3,2,1,0:T(8,128)(2,1)S(1)} %copy-done.4, f32[1536]{0:T(1024)} %copy-done.10, f32[1536]{0:T(1024)} %copy-done.11, f32[128]{0:T(128)} %copy-done.22, f32[128]{0:T(128)} %copy-done.19), kind=kOutput, calls=%fused_computation.28 | convolution fusion | flops 303267840 | bytes 2962432 | tf_op jit(solution)/shard_map/dot_general | solution.py:81
  37.7 2.1 %convolution_convert_fusion.11 = bf16[40,512]{1,0:T(8,128)(2,1)S(1)} fusion(bf16[1536,512]{0,1:T(8,128)(2,1)} %bitcast.122, bf16[1,1,40,1536]{3,2,1,0:T(8,128)(2,1)} %param.14, f32[1536]{0:T(1024)S(1)} %get-tuple-element.24, f32[1536]{0:T(1024)S(1)} %get-tuple-element.25, f32[40]{0:T(128)} %copy-done.18, f32[40]{0:T(128)} %copy-done.17), kind=kOutput, calls=%fused_computation.32 | convolution fusion | flops 63303680 | bytes 1749312 | tf_op jit(solution)/shard_map/dot_general | solution.py:86
  39.8 1.5 convolution_convert_fusion.8
  41.3 8.3 %collective-permute-done.1 = bf16[168,1536]{1,0:T(8,128)(2,1)} collective-permute-done((bf16[168,1536]{1,0:T(8,128)(2,1)}, bf16[168,1536]{1,0:T(8,128)(2,1)}, u32[]{:S(2)}, u32[]{:S(2)}) %collective-permute-start.1) | collective-permute-done | bytes 516128 | tf_op jit(solution)/shard_map/ppermute | solution.py:22
  49.6 1.5 convolution_convert_fusion.9
  51.1 1.5 convolution_convert_fusion.10
  52.6 0.7 pad_maximum_fusion.2
  53.2 1.8 copy.24
  55.0 1.8 slice_bitcast_fusion.5
  56.9 2.7 %convolution_convert_fusion.4 = bf16[128,768]{1,0:T(8,128)(2,1)S(1)} fusion(bf16[1536,768]{0,1:T(8,128)(2,1)} %bitcast.127, bf16[168,1536]{1,0:T(8,128)(2,1)} %collective-permute-done.2), kind=kOutput, calls=%fused_computation.25 | convolution fusion | flops 302088192 | bytes 2949120 | tf_op jit(solution)/shard_map/dot_general | solution.py:81
  59.5 2.7 %convolution_convert_fusion.5 = bf16[128,768]{1,0:T(8,128)(2,1)S(1)} fusion(bf16[1536,768]{0,1:T(8,128)(2,1)} %bitcast.128, bf16[168,1536]{1,0:T(8,128)(2,1)} %collective-permute-done.1), kind=kOutput, calls=%fused_computation.26 | convolution fusion | flops 302088192 | bytes 2949120 | tf_op jit(solution)/shard_map/dot_general | solution.py:81
  62.2 1.9 convolution_convert_fusion.6
  64.1 1.0 pad_maximum_fusion
  65.1 2.3 %copy.21 = bf16[512,768]{0,1:T(8,128)(2,1)} copy(bf16[512,768]{1,0:T(8,128)(2,1)} %pad_maximum_fusion) | data formatting | bytes 1572864 | tf_op jit(solution)/shard_map/concatenate | solution.py:90
  67.4 1.1 slice_bitcast_fusion.3
  68.4 2.4 %fusion = (f32[4,512]{1,0:T(4,128)S(1)}, f32[4,512,672]{1,2,0:T(8,128)S(1)}) fusion(pred[672]{0:T(1024)(128)(4,1)S(1)} %copy-done.13, bf16[160,4,64]{0,2,1:T(8,128)(2,1)} %get-tuple-element.39, bf16[512,4,64]{0,2,1:T(8,128)(2,1)S(1)} %get-tuple-element.33, bf16[512,4,3,64]{0,3,2,1:T(8,128)(2,1)} %bitcast.133), kind=kOutput, calls=%fused_computation.2 | convolution fusion | flops 180975616 | bytes 6169248 | tf_op jit(solution)/shard_map/while/body/eval_jaxpr/qhe,khe->hqk/dot_general | solution.py:107
  70.8 1.2 fusion.1
  72.0 1.4 fusion.16
  73.5 12.6 %collective-permute-start.5 = (bf16[128,256]{0,1:T(8,128)(2,1)S(1)}, bf16[128,256]{0,1:T(8,128)(2,1)S(1)}, u32[]{:S(2)}, u32[]{:S(2)}) collective-permute-start(bf16[128,256]{0,1:T(8,128)(2,1)S(1)} %bitcast.137), channel_id=1, source_target_pairs={{0,3},{1,0},{2,1},{3,2},{4,7},{5,4},{6,5},{7,6},{8,11},{9,8},{10,9... | collective-permute-start | bytes 196616 | tf_op jit(solution)/shard_map/ppermute | solution.py:22
  86.1 0.6 collective-permute-start.4
  87.0 5.1 %collective-permute-done.3 = bf16[128,256]{0,1:T(8,128)(2,1)S(1)} collective-permute-done((bf16[128,256]{0,1:T(8,128)(2,1)S(1)}, bf16[128,256]{0,1:T(8,128)(2,1)S(1)}, u32[]{:S(2)}, u32[]{:S(2)}) %collective-permute-start.3) | collective-permute-done | bytes 65568 | tf_op jit(solution)/shard_map/ppermute | solution.py:22
  93.4 0.6 copy-done.3
  94.3 0.7 collective-permute-start.10
  95.0 2.2 %collective-permute-start.8 = (bf16[128,1536]{1,0:T(8,128)(2,1)S(1)}, bf16[128,1536]{1,0:T(8,128)(2,1)}, u32[]{:S(2)}, u32[]{:S(2)}) collective-permute-start(bf16[128,1536]{1,0:T(8,128)(2,1)S(1)} %add_convert_fusion.1), channel_id=1, source_target_pairs={{0,2},{1,3},{2,0},{3,1},{4,6},{5,7},{6,4},{7,5},{8,10},{9,11},{10,... | collective-permute-start | bytes 1179656 | tf_op jit(solution)/shard_map/ppermute | solution.py:22
  97.2 1.0 collective-permute-start.6
  98.1 10.1 %collective-permute-done.10 = bf16[128,1536]{1,0:T(8,128)(2,1)} collective-permute-done((bf16[128,1536]{1,0:T(8,128)(2,1)S(1)}, bf16[128,1536]{1,0:T(8,128)(2,1)}, u32[]{:S(2)}, u32[]{:S(2)}) %collective-permute-start.10) | collective-permute-done | bytes 393248 | tf_op jit(solution)/shard_map/ppermute | solution.py:22
  108.3 6.3 %convolution_convert_fusion = bf16[128,1536]{1,0:T(8,128)(2,1)} fusion(bf16[1536,1536]{1,0:T(8,128)(2,1)} %param.19, bf16[128,1536]{1,0:T(8,128)(2,1)} %collective-permute-done.10, bf16[1536,1536]{1,0:T(8,128)(2,1)} %param.18), kind=kOutput, calls=%fused_computation.12 | convolution fusion | flops 1209925632 | bytes 10223616 | tf_op jit(solution)/shard_map/dot_general | solution.py:139
  114.6 7.3 %collective-permute-done.8 = bf16[128,1536]{1,0:T(8,128)(2,1)} collective-permute-done((bf16[128,1536]{1,0:T(8,128)(2,1)S(1)}, bf16[128,1536]{1,0:T(8,128)(2,1)}, u32[]{:S(2)}, u32[]{:S(2)}) %collective-permute-start.8) | collective-permute-done | bytes 393248 | tf_op jit(solution)/shard_map/ppermute | solution.py:22
  121.8 6.3 %convolution_convert_fusion.1 = bf16[128,1536]{1,0:T(8,128)(2,1)} fusion(bf16[1536,1536]{1,0:T(8,128)(2,1)} %param.19, bf16[128,1536]{1,0:T(8,128)(2,1)} %collective-permute-done.8, bf16[1536,1536]{1,0:T(8,128)(2,1)} %param.18), kind=kOutput, calls=%fused_computation.13 | convolution fusion | flops 1209925632 | bytes 10223616 | tf_op jit(solution)/shard_map/dot_general | solution.py:139
  128.1 20.5 %collective-permute-start.9 = (bf16[128,1536]{1,0:T(8,128)(2,1)}, bf16[128,1536]{1,0:T(8,128)(2,1)}, u32[]{:S(2)}, u32[]{:S(2)}) collective-permute-start(bf16[128,1536]{1,0:T(8,128)(2,1)} %convolution_convert_fusion.1), channel_id=1, source_target_pairs={{0,2},{1,3},{2,0},{3,1},{4,6},{5,7},{6,4},{7,5},{8,10},{9,11},{10,... | collective-permute-start | bytes 1179656 | tf_op jit(solution)/shard_map/ppermute | solution.py:22
  148.6 6.3 %convolution_convert_fusion.2 = bf16[128,1536]{1,0:T(8,128)(2,1)} fusion(bf16[1536,1536]{1,0:T(8,128)(2,1)} %param.19, bf16[128,1536]{1,0:T(8,128)(2,1)} %collective-permute-done.6, bf16[1536,1536]{1,0:T(8,128)(2,1)} %param.18), kind=kOutput, calls=%fused_computation.14 | convolution fusion | flops 1209925632 | bytes 10223616 | tf_op jit(solution)/shard_map/dot_general | solution.py:139
  154.9 2.0 %collective-permute-start.7 = (bf16[128,1536]{1,0:T(8,128)(2,1)}, bf16[128,1536]{1,0:T(8,128)(2,1)S(1)}, u32[]{:S(2)}, u32[]{:S(2)}) collective-permute-start(bf16[128,1536]{1,0:T(8,128)(2,1)} %convolution_convert_fusion.2), channel_id=1, source_target_pairs={{0,1},{1,2},{2,3},{3,0},{4,5},{5,6},{6,7},{7,4},{8,9},{9,10},{10,1... | collective-permute-start | bytes 1179656 | tf_op jit(solution)/shard_map/ppermute | solution.py:22
  156.9 12.7 %collective-permute-done.9 = bf16[128,1536]{1,0:T(8,128)(2,1)} collective-permute-done((bf16[128,1536]{1,0:T(8,128)(2,1)}, bf16[128,1536]{1,0:T(8,128)(2,1)}, u32[]{:S(2)}, u32[]{:S(2)}) %collective-permute-start.9) | collective-permute-done | bytes 393248 | tf_op jit(solution)/shard_map/ppermute | solution.py:22
  169.6 0.7 copy-done.25
  170.4 7.2 %fusion.161 = (f32[128]{0:T(128)S(1)}, f32[128,1536]{1,0:T(8,128)}) fusion(f32[128,1536]{1,0:T(8,128)} %copy-done.3, bf16[128,1536]{1,0:T(8,128)(2,1)} %collective-permute-done.11, bf16[128,1536]{1,0:T(8,128)(2,1)} %collective-permute-done.9, bf16[128,1536]{1,0:T(8,128)(2,1)} %copy-done.25, bf16[1536,1536]{1,0:T(8,128)(2,1)} %param.19, ...), kind=kOutput, calls=%fused_computation.216 | convolution fusion | flops 1212874624 | bytes 12209664 | tf_op jit(solution)/shard_map/dot_general | solution.py:139
  177.6 1.4 multiply_reduce_fusion
  179.0 1.5 fusion.162
  180.5 1.6 collective-permute-start.12
  184.3 0.6 multiply_reduce_fusion.2
  184.9 1.3 pad_maximum_fusion.3
  186.2 3.6 %collective-permute-done.13 = f32[2]{0:T(128)S(1)} collective-permute-done((f32[2]{0:T(128)S(1)}, f32[2]{0:T(128)S(1)}, u32[]{:S(2)}, u32[]{:S(2)}) %collective-permute-start.13) | collective-permute-done | bytes 40 | tf_op jit(solution)/shard_map/ppermute | solution.py:17
  189.8 1.3 fusion.196
  191.5 4.0 %collective-permute-done.14 = f32[2]{0:T(128)S(1)} collective-permute-done((f32[2]{0:T(128)S(1)}, f32[2]{0:T(128)S(1)}, u32[]{:S(2)}, u32[]{:S(2)}) %collective-permute-start.14) | collective-permute-done | bytes 40 | tf_op jit(solution)/shard_map/ppermute | solution.py:17
  195.5 1.3 fusion.197
  196.8 0.6 fusion.159
  198.8 0.6 fusion.130
  (79 shorter events, 2.6 us)
Async XLA Ops:
  0.6 86.1 %copy-start = (bf16[1024,1536]{1,0:T(8,128)(2,1)S(1)}, bf16[1024,1536]{1,0:T(8,128)(2,1)}, u32[]{:S(2)}) copy-start(bf16[1024,1536]{1,0:T(8,128)(2,1)} %param.17) | copy-start | bytes 9437188
  2.4 5.6 %copy-start.10 = (f32[1536]{0:T(1024)}, f32[1536]{0:T(1024)S(1)}, u32[]{:S(2)}) copy-start(f32[1536]{0:T(1024)S(1)} %get-tuple-element.26) | copy-start | bytes 18436
  2.4 5.6 %copy-start.11 = (f32[1536]{0:T(1024)}, f32[1536]{0:T(1024)S(1)}, u32[]{:S(2)}) copy-start(f32[1536]{0:T(1024)S(1)} %get-tuple-element.27) | copy-start | bytes 18436
  3.4 4.6 %copy-start.17 = (f32[40]{0:T(128)}, f32[40]{0:T(128)S(1)}, u32[]{:S(2)}) copy-start(f32[40]{0:T(128)S(1)} %broadcast_multiply_fusion) | copy-start | bytes 484
  4.6 3.5 %copy-start.18 = (f32[40]{0:T(128)}, f32[40]{0:T(128)S(1)}, u32[]{:S(2)}) copy-start(f32[40]{0:T(128)S(1)} %add_rsqrt_fusion.2) | copy-start | bytes 484
  5.7 2.3 %copy-start.19 = (f32[128]{0:T(128)}, f32[128]{0:T(128)S(1)}, u32[]{:S(2)}) copy-start(f32[128]{0:T(128)S(1)} %broadcast_multiply_fusion.3) | copy-start | bytes 1540
  7.0 1.1 copy-start.22
  10.2 29.6 %collective-permute-start.2 = (bf16[168,1536]{1,0:T(8,128)(2,1)}, bf16[168,1536]{1,0:T(8,128)(2,1)}, u32[]{:S(2)}, u32[]{:S(2)}) collective-permute-start(bf16[168,1536]{1,0:T(8,128)(2,1)} %pad_maximum_fusion.1), channel_id=1, source_target_pairs={{0,1},{1,2},{2,3},{3,0},{4,5},{5,6},{6,7},{7,4},{8,9},{9,10},{10,1... | collective-permute-start | bytes 1548296 | tf_op jit(solution)/shard_map/ppermute | solution.py:22
  13.2 36.3 %collective-permute-start.1 = (bf16[168,1536]{1,0:T(8,128)(2,1)}, bf16[168,1536]{1,0:T(8,128)(2,1)}, u32[]{:S(2)}, u32[]{:S(2)}) collective-permute-start(bf16[168,1536]{1,0:T(8,128)(2,1)} %pad_maximum_fusion.1), channel_id=1, source_target_pairs={{0,2},{1,3},{2,0},{3,1},{4,6},{5,7},{6,4},{7,5},{8,10},{9,11},{10,... | collective-permute-start | bytes 1548296 | tf_op jit(solution)/shard_map/ppermute | solution.py:22
  15.8 35.2 %collective-permute-start = (bf16[168,1536]{1,0:T(8,128)(2,1)}, bf16[168,1536]{1,0:T(8,128)(2,1)}, u32[]{:S(2)}, u32[]{:S(2)}) collective-permute-start(bf16[168,1536]{1,0:T(8,128)(2,1)} %pad_maximum_fusion.1), channel_id=1, source_target_pairs={{0,3},{1,0},{2,1},{3,2},{4,7},{5,4},{6,5},{7,6},{8,11},{9,8},{10,9... | collective-permute-start | bytes 1548296 | tf_op jit(solution)/shard_map/ppermute | solution.py:22
  23.5 10.9 %copy-start.4 = (bf16[1,1,128,1536]{3,2,1,0:T(8,128)(2,1)S(1)}, bf16[1,1,128,1536]{3,2,1,0:T(8,128)(2,1)}, u32[]{:S(2)}) copy-start(bf16[1,1,128,1536]{3,2,1,0:T(8,128)(2,1)} %param.13) | copy-start | bytes 1179652
  34.3 5.5 %copy-start.1 = (bf16[1536,4,2,64]{0,3,2,1:T(8,128)(2,1)S(1)}, bf16[1536,4,2,64]{0,3,2,1:T(8,128)(2,1)}, u32[]{:S(2)}) copy-start(bf16[1536,4,2,64]{0,3,2,1:T(8,128)(2,1)} %slice.135) | copy-start | bytes 4718596
  55.0 7.2 %copy-start.2 = (bf16[1536,4,3,64]{0,3,2,1:T(8,128)(2,1)S(1)}, bf16[1536,4,3,64]{0,3,2,1:T(8,128)(2,1)}, u32[]{:S(2)}) copy-start(bf16[1536,4,3,64]{0,3,2,1:T(8,128)(2,1)} %slice.130) | copy-start | bytes 7077892
  55.0 9.1 %copy-start.5 = (bf16[128,768]{1,0:T(8,128)(2,1)S(1)}, bf16[128,768]{1,0:T(8,128)(2,1)}, u32[]{:S(2)}) copy-start(bf16[128,768]{1,0:T(8,128)(2,1)} %convolution_convert_fusion.7) | copy-start | bytes 589828
  59.5 8.9 %copy-start.13 = (pred[672]{0:T(1024)(128)(4,1)S(1)}, pred[672]{0:T(1024)(128)(4,1)}, u32[]{:S(2)}) copy-start(pred[672]{0:T(1024)(128)(4,1)} %concatenate.18) | copy-start | bytes 2020
  68.4 3.6 %copy-start.6 = (bf16[160,4,64]{0,2,1:T(8,128)(2,1)S(1)}, bf16[160,4,64]{0,2,1:T(8,128)(2,1)}, u32[]{:S(2)}) copy-start(bf16[160,4,64]{0,2,1:T(8,128)(2,1)} %get-tuple-element.38) | copy-start | bytes 245764
  73.4 19.3 %copy-start.9 = (f32[1536]{0:T(1024)S(1)}, f32[1536]{0:T(1024)}, u32[]{:S(2)}) copy-start(f32[1536]{0:T(1024)} %get-tuple-element.28) | copy-start | bytes 18436
  73.5 19.0 %collective-permute-start.5 = (bf16[128,256]{0,1:T(8,128)(2,1)S(1)}, bf16[128,256]{0,1:T(8,128)(2,1)S(1)}, u32[]{:S(2)}, u32[]{:S(2)}) collective-permute-start(bf16[128,256]{0,1:T(8,128)(2,1)S(1)} %bitcast.137), channel_id=1, source_target_pairs={{0,3},{1,0},{2,1},{3,2},{4,7},{5,4},{6,5},{7,6},{8,11},{9,8},{10,9... | collective-permute-start | bytes 196616 | tf_op jit(solution)/shard_map/ppermute | solution.py:22
  86.1 6.1 %collective-permute-start.3 = (bf16[128,256]{0,1:T(8,128)(2,1)S(1)}, bf16[128,256]{0,1:T(8,128)(2,1)S(1)}, u32[]{:S(2)}, u32[]{:S(2)}) collective-permute-start(bf16[128,256]{0,1:T(8,128)(2,1)S(1)} %bitcast.138), channel_id=1, source_target_pairs={{0,1},{1,2},{2,3},{3,0},{4,5},{5,6},{6,7},{7,4},{8,9},{9,10},{10,1... | collective-permute-start | bytes 196616 | tf_op jit(solution)/shard_map/ppermute | solution.py:22
  86.1 6.7 %collective-permute-start.4 = (bf16[128,256]{0,1:T(8,128)(2,1)S(1)}, bf16[128,256]{0,1:T(8,128)(2,1)S(1)}, u32[]{:S(2)}, u32[]{:S(2)}) collective-permute-start(bf16[128,256]{0,1:T(8,128)(2,1)S(1)} %bitcast.136), channel_id=1, source_target_pairs={{0,2},{1,3},{2,0},{3,1},{4,6},{5,7},{6,4},{7,5},{8,10},{9,11},{10,... | collective-permute-start | bytes 196616 | tf_op jit(solution)/shard_map/ppermute | solution.py:22
  86.7 7.4 %copy-start.7 = (f32[1536]{0:T(1024)S(1)}, f32[1536]{0:T(1024)}, u32[]{:S(2)}) copy-start(f32[1536]{0:T(1024)} %get-tuple-element.15) | copy-start | bytes 18436
  86.7 7.4 %copy-start.8 = (f32[1536]{0:T(1024)S(1)}, f32[1536]{0:T(1024)}, u32[]{:S(2)}) copy-start(f32[1536]{0:T(1024)} %get-tuple-element.16) | copy-start | bytes 18436
  93.2 0.9 copy-start.3
  93.2 5.0 %copy-start.20 = (f32[128]{0:T(128)}, f32[128]{0:T(128)S(1)}, u32[]{:S(2)}) copy-start(f32[128]{0:T(128)S(1)} %broadcast_multiply_fusion.2) | copy-start | bytes 1540
  93.4 4.7 %copy-start.23 = (f32[128]{0:T(128)}, f32[128]{0:T(128)S(1)}, u32[]{:S(2)}) copy-start(f32[128]{0:T(128)S(1)} %add_rsqrt_fusion.1) | copy-start | bytes 1540
  94.3 14.0 %collective-permute-start.10 = (bf16[128,1536]{1,0:T(8,128)(2,1)S(1)}, bf16[128,1536]{1,0:T(8,128)(2,1)}, u32[]{:S(2)}, u32[]{:S(2)}) collective-permute-start(bf16[128,1536]{1,0:T(8,128)(2,1)S(1)} %add_convert_fusion.1), channel_id=1, source_target_pairs={{0,1},{1,2},{2,3},{3,0},{4,5},{5,6},{6,7},{7,4},{8,9},{9,10},{10,1... | collective-permute-start | bytes 1179656 | tf_op jit(solution)/shard_map/ppermute | solution.py:22
  95.0 26.9 %collective-permute-start.8 = (bf16[128,1536]{1,0:T(8,128)(2,1)S(1)}, bf16[128,1536]{1,0:T(8,128)(2,1)}, u32[]{:S(2)}, u32[]{:S(2)}) collective-permute-start(bf16[128,1536]{1,0:T(8,128)(2,1)S(1)} %add_convert_fusion.1), channel_id=1, source_target_pairs={{0,2},{1,3},{2,0},{3,1},{4,6},{5,7},{6,4},{7,5},{8,10},{9,11},{10,... | collective-permute-start | bytes 1179656 | tf_op jit(solution)/shard_map/ppermute | solution.py:22
  97.2 51.4 %collective-permute-start.6 = (bf16[128,1536]{1,0:T(8,128)(2,1)S(1)}, bf16[128,1536]{1,0:T(8,128)(2,1)}, u32[]{:S(2)}, u32[]{:S(2)}) collective-permute-start(bf16[128,1536]{1,0:T(8,128)(2,1)S(1)} %add_convert_fusion.1), channel_id=1, source_target_pairs={{0,3},{1,0},{2,1},{3,2},{4,7},{5,4},{6,5},{7,6},{8,11},{9,8},{10,9... | collective-permute-start | bytes 1179656 | tf_op jit(solution)/shard_map/ppermute | solution.py:22
  114.5 42.4 %collective-permute-start.11 = (bf16[128,1536]{1,0:T(8,128)(2,1)}, bf16[128,1536]{1,0:T(8,128)(2,1)}, u32[]{:S(2)}, u32[]{:S(2)}) collective-permute-start(bf16[128,1536]{1,0:T(8,128)(2,1)} %convolution_convert_fusion), channel_id=1, source_target_pairs={{0,3},{1,0},{2,1},{3,2},{4,7},{5,4},{6,5},{7,6},{8,11},{9,8},{10,9... | collective-permute-start | bytes 1179656 | tf_op jit(solution)/shard_map/ppermute | solution.py:22
  128.1 41.5 %collective-permute-start.9 = (bf16[128,1536]{1,0:T(8,128)(2,1)}, bf16[128,1536]{1,0:T(8,128)(2,1)}, u32[]{:S(2)}, u32[]{:S(2)}) collective-permute-start(bf16[128,1536]{1,0:T(8,128)(2,1)} %convolution_convert_fusion.1), channel_id=1, source_target_pairs={{0,2},{1,3},{2,0},{3,1},{4,6},{5,7},{6,4},{7,5},{8,10},{9,11},{10,... | collective-permute-start | bytes 1179656 | tf_op jit(solution)/shard_map/ppermute | solution.py:22
  148.6 21.8 %copy-start.16 = (f32[1536]{0:T(1024)S(1)}, f32[1536]{0:T(1024)}, u32[]{:S(2)}) copy-start(f32[1536]{0:T(1024)} %get-tuple-element.17) | copy-start | bytes 18436
  148.6 21.8 %copy-start.21 = (f32[128]{0:T(128)S(1)}, f32[128]{0:T(128)}, u32[]{:S(2)}) copy-start(f32[128]{0:T(128)} %copy-done.20) | copy-start | bytes 1540
  148.6 21.8 %copy-start.24 = (f32[128]{0:T(128)S(1)}, f32[128]{0:T(128)}, u32[]{:S(2)}) copy-start(f32[128]{0:T(128)} %copy-done.23) | copy-start | bytes 1540
  154.9 14.7 %collective-permute-start.7 = (bf16[128,1536]{1,0:T(8,128)(2,1)}, bf16[128,1536]{1,0:T(8,128)(2,1)S(1)}, u32[]{:S(2)}, u32[]{:S(2)}) collective-permute-start(bf16[128,1536]{1,0:T(8,128)(2,1)} %convolution_convert_fusion.2), channel_id=1, source_target_pairs={{0,1},{1,2},{2,3},{3,0},{4,5},{5,6},{6,7},{7,4},{8,9},{9,10},{10,1... | collective-permute-start | bytes 1179656 | tf_op jit(solution)/shard_map/ppermute | solution.py:22
  169.6 0.7 copy-start.25
  170.3 8.6 %copy-start.14 = (f32[1536]{0:T(1024)S(1)}, f32[1536]{0:T(1024)}, u32[]{:S(2)}) copy-start(f32[1536]{0:T(1024)} %get-tuple-element.14) | copy-start | bytes 18436
  170.3 8.6 %copy-start.15 = (f32[1536]{0:T(1024)S(1)}, f32[1536]{0:T(1024)}, u32[]{:S(2)}) copy-start(f32[1536]{0:T(1024)} %get-tuple-element.29) | copy-start | bytes 18436
  170.4 8.6 %copy-start.26 = (bf16[64,1536]{1,0:T(8,128)(2,1)S(1)}, bf16[64,1536]{1,0:T(8,128)(2,1)}, u32[]{:S(2)}) copy-start(bf16[64,1536]{1,0:T(8,128)(2,1)} %param.20) | copy-start | bytes 589828
  170.4 28.4 %copy-start.12 = (f32[1,32,128]{2,1,0:T(8,128)S(1)}, f32[1,32,128]{2,1,0:T(8,128)}, u32[]{:S(2)}) copy-start(f32[1,32,128]{2,1,0:T(8,128)} %param.21) | copy-start | bytes 49156
  180.5 3.8 %collective-permute-start.12 = (bf16[64,128]{1,0:T(8,128)(2,1)S(1)}, bf16[64,128]{1,0:T(8,128)(2,1)S(1)}, u32[]{:S(2)}, u32[]{:S(2)}) collective-permute-start(bf16[64,128]{1,0:T(8,128)(2,1)S(1)} %get-tuple-element.51), channel_id=1, source_target_pairs={{0,16},{16,0},{1,17},{17,1},{2,18},{18,2},{3,19},{19,3},{4,20},{20... | collective-permute-start | bytes 49160 | tf_op jit(solution)/shard_map/ppermute | solution.py:17
  186.2 3.6 %collective-permute-start.13 = (f32[2]{0:T(128)S(1)}, f32[2]{0:T(128)S(1)}, u32[]{:S(2)}, u32[]{:S(2)}) collective-permute-start(f32[2]{0:T(128)S(1)} %pad_maximum_fusion.3), channel_id=1, source_target_pairs={{0,1},{1,0},{2,3},{3,2},{4,5},{5,4},{6,7},{7,6},{8,9},{9,8},{10,11... | collective-permute-start | bytes 32 | tf_op jit(solution)/shard_map/ppermute | solution.py:17
  191.0 4.5 %collective-permute-start.14 = (f32[2]{0:T(128)S(1)}, f32[2]{0:T(128)S(1)}, u32[]{:S(2)}, u32[]{:S(2)}) collective-permute-start(f32[2]{0:T(128)S(1)} %fusion.196), channel_id=1, source_target_pairs={{0,2},{1,3},{2,0},{3,1},{4,6},{5,7},{6,4},{7,5},{8,10},{9,11},{10,... | collective-permute-start | bytes 32 | tf_op jit(solution)/shard_map/ppermute | solution.py:17

commit v5 on v2

--- a/solution.py
+++ b/solution.py
@@ -145,8 +145,9 @@
     uncond_vel = jnp.where(leading, partner_vel, own_vel)
     guided = uncond_vel + guidance[0] * (cond_vel - uncond_vel)
     squares = jnp.stack([jnp.sum(cond_vel * cond_vel), jnp.sum(guided * guided)])
-    for bit in range(seq_size.bit_length() - 1):
-        squares = squares + partner(squares, "seq", bit)
+    squares = sum(
+        [squares] + [shifted(squares, "seq", k) for k in range(1, seq_size)], jnp.zeros(2)
+    )
     cond_sq, guided_sq = squares[0], squares[1]
     entries = own_vel.shape[0] * image_total
     rms_cond = jnp.sqrt(cond_sq / entries + EPS_NORM)

time: 199 us -> 195 us (0.980)
  waiting for transfers between devices: 61.2 us -> 56 us
  starting transfers between devices: 50.2 us -> 53.3 us
    ppermute x3 -> x1, waiting for transfers between devices: 7.49 us -> 0.16 us  [partner(): return lax.ppermute(value, axis, pairs)]
    ppermute x12 -> x15, starting transfers between devices: 47.9 us -> 51.7 us  [shifted(): lax.ppermute(value, axis, [(source, (source - shift) % size) for source i...]
    ppermute x12 -> x15, waiting for transfers between devices: 53.7 us -> 55.8 us  [shifted(): lax.ppermute(value, axis, [(source, (source - shift) % size) for source i...]
  transfers between devices with their start and end apart: 15 -> 16, of which waited for: 9 -> 9; matrix products, arithmetic and copies ran while one was open for 17% -> 17% of each run, Pallas kernels for 0% -> 0%
where the time goes in v5:
time: 195 us; the launch traced here: 194 us
  waiting for transfers between devices  56 us (29%)
  starting transfers between devices  53.3 us (27%)
  matrix products  37.9 us (19%)
  local copies, waits for them, and re-layouts  21.5 us (11%)
  other arithmetic  20.7 us (11%)
  between operations  5 us (3%)
    ppermute x15, waiting for transfers between devices, shifted(): lax.ppermute(value, axis, [(source, (source - shift) % size) for source i...  55.8 us
    ppermute x15, starting transfers between devices, shifted(): lax.ppermute(value, axis, [(source, (source - shift) % size) for source i...  51.7 us
    dot_general x4, matrix products, local(): jnp.dot(inner, mlp_out_weight, preferred_element_type=jnp.float32)  26.1 us
    unnamed x35, local copies, waits for them, and re-layouts  7.69 us
    another operation x2, other arithmetic, local(): jnp.stack([own_norm] + [shifted(own_norm, 'seq', k) for k in range(1, seq...  4.14 us
    dot_general x1, matrix products, local(): jnp.dot(image_all, image_cols, preferred_element_type=jnp.float32)  3.97 us
    reduce_sum x4, other arithmetic, modulate(): spread = jnp.mean(jnp.square(values - center), axis=-1, keepdims=True)  3.94 us
  transfers between devices with their start and end apart: 16, of which 9 were waited for; matrix products, arithmetic and copies ran while one was open for 17% of the time, Pallas kernels for 0%

profile of v5, /device:TPU:0, one launch (start us, length us, event | category | flops | bytes accessed | tf_op | source)
XLA Modules:
  0.0 194.4 jit_solution(15865910571130324121)
XLA Ops:
  0.6 1.7 add_reduce_fusion
  2.4 1.0 convert_reduce_fusion.1
  3.4 1.1 fusion.100
  4.5 1.1 convert_reduce_fusion
  5.7 1.2 fusion.22
  6.9 1.0 fusion.103
  8.0 1.3 fusion.25
  9.3 1.0 fusion.132
  10.3 3.1 %collective-permute-start.2 = (bf16[168,1536]{1,0:T(8,128)(2,1)}, bf16[168,1536]{1,0:T(8,128)(2,1)}, u32[]{:S(2)}, u32[]{:S(2)}) collective-permute-start(bf16[168,1536]{1,0:T(8,128)(2,1)} %get-tuple-element.35), channel_id=1, source_target_pairs={{0,1},{1,2},{2,3},{3,0},{4,5},{5,6},{6,7},{7,4},{8,9},{9,10},{10,1... | collective-permute-start | bytes 1548296 | tf_op jit(solution)/shard_map/ppermute | solution.py:22
  13.4 2.6 %collective-permute-start.1 = (bf16[168,1536]{1,0:T(8,128)(2,1)}, bf16[168,1536]{1,0:T(8,128)(2,1)}, u32[]{:S(2)}, u32[]{:S(2)}) collective-permute-start(bf16[168,1536]{1,0:T(8,128)(2,1)} %get-tuple-element.35), channel_id=1, source_target_pairs={{0,2},{1,3},{2,0},{3,1},{4,6},{5,7},{6,4},{7,5},{8,10},{9,11},{10,... | collective-permute-start | bytes 1548296 | tf_op jit(solution)/shard_map/ppermute | solution.py:22
  16.0 1.3 collective-permute-start
  17.3 6.3 %copy.20 = bf16[1536,1280]{0,1:T(8,128)(2,1)} copy(bf16[1536,1280]{1,0:T(8,128)(2,1)} %param.16) | data formatting | bytes 7864320 | tf_op args[3]
  23.6 2.7 %slice.117 = bf16[1536,4,2,64]{0,3,2,1:T(8,128)(2,1)} slice(bf16[1536,4,5,64]{0,3,2,1:T(8,128)(2,1)} %bitcast.119), slice={[0:1536], [0:4], [3:5], [0:64]} | slice | bytes 3145728 | tf_op jit(solution)/shard_map/slice | solution.py:44
  26.2 3.2 %slice.115 = bf16[1536,4,3,64]{0,3,2,1:T(8,128)(2,1)} slice(bf16[1536,4,5,64]{0,3,2,1:T(8,128)(2,1)} %bitcast.120), slice={[0:1536], [0:4], [0:3], [0:64]} | slice | bytes 4718592 | tf_op jit(solution)/shard_map/slice | solution.py:43
  30.3 0.6 concatenate.12
  30.9 18.8 %collective-permute-done.1 = bf16[168,1536]{1,0:T(8,128)(2,1)} collective-permute-done((bf16[168,1536]{1,0:T(8,128)(2,1)}, bf16[168,1536]{1,0:T(8,128)(2,1)}, u32[]{:S(2)}, u32[]{:S(2)}) %collective-permute-start.1) | collective-permute-done | bytes 516128 | tf_op jit(solution)/shard_map/ppermute | solution.py:22
  49.7 1.1 pad_maximum_fusion.2
  50.8 3.1 %pad_maximum_fusion = bf16[4,168,1536]{2,1,0:T(8,128)(2,1)} fusion(bf16[1,168,1536]{2,1,0:T(8,128)(2,1)} %bitcast.6, bf16[1,168,1536]{2,1,0:T(8,128)(2,1)} %bitcast.5, bf16[1,168,1536]{2,1,0:T(8,128)(2,1)} %bitcast.4, bf16[1,168,1536]{2,1,0:T(8,128)(2,1)} %get-tuple-element.34), kind=kLoop, calls=%fused_computation.17 | loop fusion | flops 3096576 | bytes 4128768 | tf_op jit(solution)/shard_map/stack | solution.py:75
  53.9 1.3 convolution_convert_fusion.5
  55.3 1.0 copy.24
  56.3 0.7 slice_bitcast_fusion.5
  57.0 1.5 slice.114
  58.5 4.0 %convolution_convert_fusion.4 = bf16[512,768]{1,0:T(8,128)(2,1)} fusion(bf16[512,1536]{1,0:T(8,128)(2,1)S(1)} %bitcast.126, bf16[1536,768]{0,1:T(8,128)(2,1)} %bitcast.124), kind=kOutput, calls=%fused_computation.18 | convolution fusion | flops 1208352768 | bytes 4718592 | tf_op jit(solution)/shard_map/dot_general | solution.py:79
  62.5 2.3 %copy.21 = bf16[512,768]{0,1:T(8,128)(2,1)} copy(bf16[512,768]{1,0:T(8,128)(2,1)} %convolution_convert_fusion.4) | data formatting | bytes 1572864 | tf_op jit(solution)/shard_map/convert_element_type | solution.py:79
  64.8 1.1 slice_bitcast_fusion.3
  65.9 2.4 %fusion = (f32[4,512]{1,0:T(4,128)S(1)}, f32[4,512,672]{1,2,0:T(8,128)S(1)}) fusion(pred[672]{0:T(1024)(128)(4,1)S(1)} %copy-done.7, bf16[160,4,64]{0,2,1:T(8,128)(2,1)S(1)} %get-tuple-element.41, bf16[512,4,64]{0,2,1:T(8,128)(2,1)S(1)} %get-tuple-element.33, bf16[512,4,3,64]{0,3,2,1:T(8,128)(2,1)} %bitcast.123), kind=kOutput, calls=%fused_computation.2 | convolution fusion | flops 180975616 | bytes 6120096 | tf_op jit(solution)/shard_map/while/body/eval_jaxpr/qhe,khe->hqk/dot_general | solution.py:100
  68.2 1.2 fusion.1
  69.4 1.4 fusion.16
  70.9 12.6 %collective-permute-start.5 = (bf16[128,256]{0,1:T(8,128)(2,1)S(1)}, bf16[128,256]{0,1:T(8,128)(2,1)S(1)}, u32[]{:S(2)}, u32[]{:S(2)}) collective-permute-start(bf16[128,256]{0,1:T(8,128)(2,1)S(1)} %bitcast.130), channel_id=1, source_target_pairs={{0,3},{1,0},{2,1},{3,2},{4,7},{5,4},{6,5},{7,6},{8,11},{9,8},{10,9... | collective-permute-start | bytes 196616 | tf_op jit(solution)/shard_map/ppermute | solution.py:22
  83.5 0.6 collective-permute-start.4
  84.1 0.3 fusion.62
  84.4 5.2 %collective-permute-done.3 = bf16[128,256]{0,1:T(8,128)(2,1)S(1)} collective-permute-done((bf16[128,256]{0,1:T(8,128)(2,1)S(1)}, bf16[128,256]{0,1:T(8,128)(2,1)S(1)}, u32[]{:S(2)}, u32[]{:S(2)}) %collective-permute-start.3) | collective-permute-done | bytes 65568 | tf_op jit(solution)/shard_map/ppermute | solution.py:22
  89.6 0.3 convolution_add_fusion.1
  89.9 0.3 fusion.58
  90.3 0.4 fusion.135
  90.8 0.2 multiply_reduce_fusion.1
  91.0 0.6 copy-done.1
  91.7 0.2 add_convert_fusion.1
  91.9 0.6 collective-permute-start.10
  92.5 2.1 %collective-permute-start.8 = (bf16[128,1536]{1,0:T(8,128)(2,1)S(1)}, bf16[128,1536]{1,0:T(8,128)(2,1)}, u32[]{:S(2)}, u32[]{:S(2)}) collective-permute-start(bf16[128,1536]{1,0:T(8,128)(2,1)S(1)} %add_convert_fusion.1), channel_id=1, source_target_pairs={{0,2},{1,3},{2,0},{3,1},{4,6},{5,7},{6,4},{7,5},{8,10},{9,11},{10,... | collective-permute-start | bytes 1179656 | tf_op jit(solution)/shard_map/ppermute | solution.py:22
  94.6 1.3 collective-permute-start.6
  95.9 10.0 %collective-permute-done.10 = bf16[128,1536]{1,0:T(8,128)(2,1)} collective-permute-done((bf16[128,1536]{1,0:T(8,128)(2,1)S(1)}, bf16[128,1536]{1,0:T(8,128)(2,1)}, u32[]{:S(2)}, u32[]{:S(2)}) %collective-permute-start.10) | collective-permute-done | bytes 393248 | tf_op jit(solution)/shard_map/ppermute | solution.py:22
  105.9 6.3 %convolution_convert_fusion = bf16[128,1536]{1,0:T(8,128)(2,1)} fusion(bf16[1536,1536]{1,0:T(8,128)(2,1)} %param.19, bf16[128,1536]{1,0:T(8,128)(2,1)} %collective-permute-done.10, bf16[1536,1536]{1,0:T(8,128)(2,1)} %param.18), kind=kOutput, calls=%fused_computation.12 | convolution fusion | flops 1209925632 | bytes 10223616 | tf_op jit(solution)/shard_map/dot_general | solution.py:132
  112.2 0.8 collective-permute-start.11
  113.0 7.1 %collective-permute-done.8 = bf16[128,1536]{1,0:T(8,128)(2,1)} collective-permute-done((bf16[128,1536]{1,0:T(8,128)(2,1)S(1)}, bf16[128,1536]{1,0:T(8,128)(2,1)}, u32[]{:S(2)}, u32[]{:S(2)}) %collective-permute-start.8) | collective-permute-done | bytes 393248 | tf_op jit(solution)/shard_map/ppermute | solution.py:22
  120.0 6.3 %convolution_convert_fusion.1 = bf16[128,1536]{1,0:T(8,128)(2,1)} fusion(bf16[1536,1536]{1,0:T(8,128)(2,1)} %param.19, bf16[128,1536]{1,0:T(8,128)(2,1)} %collective-permute-done.8, bf16[1536,1536]{1,0:T(8,128)(2,1)} %param.18), kind=kOutput, calls=%fused_computation.13 | convolution fusion | flops 1209925632 | bytes 10223616 | tf_op jit(solution)/shard_map/dot_general | solution.py:132
  126.3 20.8 %collective-permute-start.9 = (bf16[128,1536]{1,0:T(8,128)(2,1)}, bf16[128,1536]{1,0:T(8,128)(2,1)}, u32[]{:S(2)}, u32[]{:S(2)}) collective-permute-start(bf16[128,1536]{1,0:T(8,128)(2,1)} %convolution_convert_fusion.1), channel_id=1, source_target_pairs={{0,2},{1,3},{2,0},{3,1},{4,6},{5,7},{6,4},{7,5},{8,10},{9,11},{10,... | collective-permute-start | bytes 1179656 | tf_op jit(solution)/shard_map/ppermute | solution.py:22
  147.2 6.3 %convolution_convert_fusion.2 = bf16[128,1536]{1,0:T(8,128)(2,1)} fusion(bf16[1536,1536]{1,0:T(8,128)(2,1)} %param.19, bf16[128,1536]{1,0:T(8,128)(2,1)} %collective-permute-done.6, bf16[1536,1536]{1,0:T(8,128)(2,1)} %param.18), kind=kOutput, calls=%fused_computation.14 | convolution fusion | flops 1209925632 | bytes 10223616 | tf_op jit(solution)/shard_map/dot_general | solution.py:132
  153.5 2.0 %collective-permute-start.7 = (bf16[128,1536]{1,0:T(8,128)(2,1)}, bf16[128,1536]{1,0:T(8,128)(2,1)S(1)}, u32[]{:S(2)}, u32[]{:S(2)}) collective-permute-start(bf16[128,1536]{1,0:T(8,128)(2,1)} %convolution_convert_fusion.2), channel_id=1, source_target_pairs={{0,1},{1,2},{2,3},{3,0},{4,5},{5,6},{6,7},{7,4},{8,9},{9,10},{10,1... | collective-permute-start | bytes 1179656 | tf_op jit(solution)/shard_map/ppermute | solution.py:22
  155.5 12.5 %collective-permute-done.9 = bf16[128,1536]{1,0:T(8,128)(2,1)} collective-permute-done((bf16[128,1536]{1,0:T(8,128)(2,1)}, bf16[128,1536]{1,0:T(8,128)(2,1)}, u32[]{:S(2)}, u32[]{:S(2)}) %collective-permute-start.9) | collective-permute-done | bytes 393248 | tf_op jit(solution)/shard_map/ppermute | solution.py:22
  168.0 0.7 copy-done.15
  168.8 7.2 %fusion.136 = (f32[128]{0:T(128)S(1)}, f32[128,1536]{1,0:T(8,128)}) fusion(f32[128,1536]{1,0:T(8,128)} %copy-done.1, bf16[128,1536]{1,0:T(8,128)(2,1)} %collective-permute-done.11, bf16[128,1536]{1,0:T(8,128)(2,1)} %collective-permute-done.9, bf16[128,1536]{1,0:T(8,128)(2,1)} %copy-done.15, bf16[1536,1536]{1,0:T(8,128)(2,1)} %param.19, ...), kind=kOutput, calls=%fused_computation.186 | convolution fusion | flops 1212874624 | bytes 12209664 | tf_op jit(solution)/shard_map/dot_general | solution.py:132
  176.0 1.4 multiply_reduce_fusion
  177.4 1.5 fusion.137
  178.9 1.6 collective-permute-start.12
  182.7 0.6 multiply_reduce_fusion.2
  183.3 1.3 pad_maximum_fusion.3
  184.6 0.8 collective-permute-start.14
  185.3 3.1 %collective-permute-start.13 = (f32[2]{0:T(128)S(1)}, f32[2]{0:T(128)S(1)}, u32[]{:S(2)}, u32[]{:S(2)}) collective-permute-start(f32[2]{0:T(128)S(1)} %pad_maximum_fusion.3), channel_id=1, source_target_pairs={{0,3},{1,0},{2,1},{3,2},{4,7},{5,4},{6,5},{7,6},{8,11},{9,8},{10,9... | collective-permute-start | bytes 32 | tf_op jit(solution)/shard_map/ppermute | solution.py:22
  188.4 1.5 collective-permute-done.15
  189.9 0.6 collective-permute-done.13
  190.5 1.3 add_add_fusion
  191.8 0.6 fusion.134
  193.8 0.6 fusion.104
  (55 shorter events, 0.6 us)
Async XLA Ops:
  0.6 83.5 %copy-start = (bf16[1024,1536]{1,0:T(8,128)(2,1)S(1)}, bf16[1024,1536]{1,0:T(8,128)(2,1)}, u32[]{:S(2)}) copy-start(bf16[1024,1536]{1,0:T(8,128)(2,1)} %param.17) | copy-start | bytes 9437188
  10.3 20.6 %collective-permute-start.2 = (bf16[168,1536]{1,0:T(8,128)(2,1)}, bf16[168,1536]{1,0:T(8,128)(2,1)}, u32[]{:S(2)}, u32[]{:S(2)}) collective-permute-start(bf16[168,1536]{1,0:T(8,128)(2,1)} %get-tuple-element.35), channel_id=1, source_target_pairs={{0,1},{1,2},{2,3},{3,0},{4,5},{5,6},{6,7},{7,4},{8,9},{9,10},{10,1... | collective-permute-start | bytes 1548296 | tf_op jit(solution)/shard_map/ppermute | solution.py:22
  13.4 36.3 %collective-permute-start.1 = (bf16[168,1536]{1,0:T(8,128)(2,1)}, bf16[168,1536]{1,0:T(8,128)(2,1)}, u32[]{:S(2)}, u32[]{:S(2)}) collective-permute-start(bf16[168,1536]{1,0:T(8,128)(2,1)} %get-tuple-element.35), channel_id=1, source_target_pairs={{0,2},{1,3},{2,0},{3,1},{4,6},{5,7},{6,4},{7,5},{8,10},{9,11},{10,... | collective-permute-start | bytes 1548296 | tf_op jit(solution)/shard_map/ppermute | solution.py:22
  16.0 33.8 %collective-permute-start = (bf16[168,1536]{1,0:T(8,128)(2,1)}, bf16[168,1536]{1,0:T(8,128)(2,1)}, u32[]{:S(2)}, u32[]{:S(2)}) collective-permute-start(bf16[168,1536]{1,0:T(8,128)(2,1)} %get-tuple-element.35), channel_id=1, source_target_pairs={{0,3},{1,0},{2,1},{3,2},{4,7},{5,4},{6,5},{7,6},{8,11},{9,8},{10,9... | collective-permute-start | bytes 1548296 | tf_op jit(solution)/shard_map/ppermute | solution.py:22
  30.9 23.0 %copy-start.2 = (bf16[1536,4,2,64]{0,3,2,1:T(8,128)(2,1)S(1)}, bf16[1536,4,2,64]{0,3,2,1:T(8,128)(2,1)}, u32[]{:S(2)}) copy-start(bf16[1536,4,2,64]{0,3,2,1:T(8,128)(2,1)} %slice.117) | copy-start | bytes 4718596
  58.5 7.4 %copy-start.7 = (pred[672]{0:T(1024)(128)(4,1)S(1)}, pred[672]{0:T(1024)(128)(4,1)}, u32[]{:S(2)}) copy-start(pred[672]{0:T(1024)(128)(4,1)} %concatenate.12) | copy-start | bytes 2020
  65.9 3.5 %copy-start.4 = (bf16[160,4,64]{0,2,1:T(8,128)(2,1)S(1)}, bf16[160,4,64]{0,2,1:T(8,128)(2,1)}, u32[]{:S(2)}) copy-start(bf16[160,4,64]{0,2,1:T(8,128)(2,1)} %get-tuple-element.40) | copy-start | bytes 245764
  70.8 19.6 %copy-start.3 = (bf16[1,1,128,1536]{3,2,1,0:T(8,128)(2,1)S(1)}, bf16[1,1,128,1536]{3,2,1,0:T(8,128)(2,1)}, u32[]{:S(2)}) copy-start(bf16[1,1,128,1536]{3,2,1,0:T(8,128)(2,1)} %param.13) | copy-start | bytes 1179652
  70.8 19.5 %copy-start.5 = (f32[1536]{0:T(1024)S(1)}, f32[1536]{0:T(1024)}, u32[]{:S(2)}) copy-start(f32[1536]{0:T(1024)} %get-tuple-element.28) | copy-start | bytes 18436
  70.9 19.1 %collective-permute-start.5 = (bf16[128,256]{0,1:T(8,128)(2,1)S(1)}, bf16[128,256]{0,1:T(8,128)(2,1)S(1)}, u32[]{:S(2)}, u32[]{:S(2)}) collective-permute-start(bf16[128,256]{0,1:T(8,128)(2,1)S(1)} %bitcast.130), channel_id=1, source_target_pairs={{0,3},{1,0},{2,1},{3,2},{4,7},{5,4},{6,5},{7,6},{8,11},{9,8},{10,9... | collective-permute-start | bytes 196616 | tf_op jit(solution)/shard_map/ppermute | solution.py:22
  83.5 6.2 %collective-permute-start.3 = (bf16[128,256]{0,1:T(8,128)(2,1)S(1)}, bf16[128,256]{0,1:T(8,128)(2,1)S(1)}, u32[]{:S(2)}, u32[]{:S(2)}) collective-permute-start(bf16[128,256]{0,1:T(8,128)(2,1)S(1)} %bitcast.131), channel_id=1, source_target_pairs={{0,1},{1,2},{2,3},{3,0},{4,5},{5,6},{6,7},{7,4},{8,9},{9,10},{10,1... | collective-permute-start | bytes 196616 | tf_op jit(solution)/shard_map/ppermute | solution.py:22
  83.5 6.9 %collective-permute-start.4 = (bf16[128,256]{0,1:T(8,128)(2,1)S(1)}, bf16[128,256]{0,1:T(8,128)(2,1)S(1)}, u32[]{:S(2)}, u32[]{:S(2)}) collective-permute-start(bf16[128,256]{0,1:T(8,128)(2,1)S(1)} %bitcast.129), channel_id=1, source_target_pairs={{0,2},{1,3},{2,0},{3,1},{4,6},{5,7},{6,4},{7,5},{8,10},{9,11},{10,... | collective-permute-start | bytes 196616 | tf_op jit(solution)/shard_map/ppermute | solution.py:22
  90.8 0.9 copy-start.1
  90.8 5.1 %copy-start.11 = (f32[128]{0:T(128)}, f32[128]{0:T(128)S(1)}, u32[]{:S(2)}) copy-start(f32[128]{0:T(128)S(1)} %broadcast_multiply_fusion.2) | copy-start | bytes 1540
  91.0 4.9 %copy-start.13 = (f32[128]{0:T(128)}, f32[128]{0:T(128)S(1)}, u32[]{:S(2)}) copy-start(f32[128]{0:T(128)S(1)} %add_rsqrt_fusion.1) | copy-start | bytes 1540
  91.9 14.0 %collective-permute-start.10 = (bf16[128,1536]{1,0:T(8,128)(2,1)S(1)}, bf16[128,1536]{1,0:T(8,128)(2,1)}, u32[]{:S(2)}, u32[]{:S(2)}) collective-permute-start(bf16[128,1536]{1,0:T(8,128)(2,1)S(1)} %add_convert_fusion.1), channel_id=1, source_target_pairs={{0,1},{1,2},{2,3},{3,0},{4,5},{5,6},{6,7},{7,4},{8,9},{9,10},{10,1... | collective-permute-start | bytes 1179656 | tf_op jit(solution)/shard_map/ppermute | solution.py:22
  92.5 27.6 %collective-permute-start.8 = (bf16[128,1536]{1,0:T(8,128)(2,1)S(1)}, bf16[128,1536]{1,0:T(8,128)(2,1)}, u32[]{:S(2)}, u32[]{:S(2)}) collective-permute-start(bf16[128,1536]{1,0:T(8,128)(2,1)S(1)} %add_convert_fusion.1), channel_id=1, source_target_pairs={{0,2},{1,3},{2,0},{3,1},{4,6},{5,7},{6,4},{7,5},{8,10},{9,11},{10,... | collective-permute-start | bytes 1179656 | tf_op jit(solution)/shard_map/ppermute | solution.py:22
  94.6 52.6 %collective-permute-start.6 = (bf16[128,1536]{1,0:T(8,128)(2,1)S(1)}, bf16[128,1536]{1,0:T(8,128)(2,1)}, u32[]{:S(2)}, u32[]{:S(2)}) collective-permute-start(bf16[128,1536]{1,0:T(8,128)(2,1)S(1)} %add_convert_fusion.1), channel_id=1, source_target_pairs={{0,3},{1,0},{2,1},{3,2},{4,7},{5,4},{6,5},{7,6},{8,11},{9,8},{10,9... | collective-permute-start | bytes 1179656 | tf_op jit(solution)/shard_map/ppermute | solution.py:22
  112.2 43.3 %collective-permute-start.11 = (bf16[128,1536]{1,0:T(8,128)(2,1)}, bf16[128,1536]{1,0:T(8,128)(2,1)}, u32[]{:S(2)}, u32[]{:S(2)}) collective-permute-start(bf16[128,1536]{1,0:T(8,128)(2,1)} %convolution_convert_fusion), channel_id=1, source_target_pairs={{0,3},{1,0},{2,1},{3,2},{4,7},{5,4},{6,5},{7,6},{8,11},{9,8},{10,9... | collective-permute-start | bytes 1179656 | tf_op jit(solution)/shard_map/ppermute | solution.py:22
  126.3 41.7 %collective-permute-start.9 = (bf16[128,1536]{1,0:T(8,128)(2,1)}, bf16[128,1536]{1,0:T(8,128)(2,1)}, u32[]{:S(2)}, u32[]{:S(2)}) collective-permute-start(bf16[128,1536]{1,0:T(8,128)(2,1)} %convolution_convert_fusion.1), channel_id=1, source_target_pairs={{0,2},{1,3},{2,0},{3,1},{4,6},{5,7},{6,4},{7,5},{8,10},{9,11},{10,... | collective-permute-start | bytes 1179656 | tf_op jit(solution)/shard_map/ppermute | solution.py:22
  147.1 21.6 %copy-start.10 = (f32[1536]{0:T(1024)S(1)}, f32[1536]{0:T(1024)}, u32[]{:S(2)}) copy-start(f32[1536]{0:T(1024)} %get-tuple-element.17) | copy-start | bytes 18436
  147.1 21.6 %copy-start.12 = (f32[128]{0:T(128)S(1)}, f32[128]{0:T(128)}, u32[]{:S(2)}) copy-start(f32[128]{0:T(128)} %copy-done.11) | copy-start | bytes 1540
  147.1 21.6 %copy-start.14 = (f32[128]{0:T(128)S(1)}, f32[128]{0:T(128)}, u32[]{:S(2)}) copy-start(f32[128]{0:T(128)} %copy-done.13) | copy-start | bytes 1540
  153.5 14.5 %collective-permute-start.7 = (bf16[128,1536]{1,0:T(8,128)(2,1)}, bf16[128,1536]{1,0:T(8,128)(2,1)S(1)}, u32[]{:S(2)}, u32[]{:S(2)}) collective-permute-start(bf16[128,1536]{1,0:T(8,128)(2,1)} %convolution_convert_fusion.2), channel_id=1, source_target_pairs={{0,1},{1,2},{2,3},{3,0},{4,5},{5,6},{6,7},{7,4},{8,9},{9,10},{10,1... | collective-permute-start | bytes 1179656 | tf_op jit(solution)/shard_map/ppermute | solution.py:22
  168.0 0.7 copy-start.15
  168.7 8.6 %copy-start.8 = (f32[1536]{0:T(1024)S(1)}, f32[1536]{0:T(1024)}, u32[]{:S(2)}) copy-start(f32[1536]{0:T(1024)} %get-tuple-element.14) | copy-start | bytes 18436
  168.7 8.6 %copy-start.9 = (f32[1536]{0:T(1024)S(1)}, f32[1536]{0:T(1024)}, u32[]{:S(2)}) copy-start(f32[1536]{0:T(1024)} %get-tuple-element.29) | copy-start | bytes 18436
  168.7 8.6 %copy-start.16 = (bf16[64,1536]{1,0:T(8,128)(2,1)S(1)}, bf16[64,1536]{1,0:T(8,128)(2,1)}, u32[]{:S(2)}) copy-start(bf16[64,1536]{1,0:T(8,128)(2,1)} %param.20) | copy-start | bytes 589828
  168.8 25.0 %copy-start.6 = (f32[1,32,128]{2,1,0:T(8,128)S(1)}, f32[1,32,128]{2,1,0:T(8,128)}, u32[]{:S(2)}) copy-start(f32[1,32,128]{2,1,0:T(8,128)} %param.21) | copy-start | bytes 49156
  178.9 3.8 %collective-permute-start.12 = (bf16[64,128]{1,0:T(8,128)(2,1)S(1)}, bf16[64,128]{1,0:T(8,128)(2,1)S(1)}, u32[]{:S(2)}, u32[]{:S(2)}) collective-permute-start(bf16[64,128]{1,0:T(8,128)(2,1)S(1)} %get-tuple-element.53), channel_id=1, source_target_pairs={{0,16},{16,0},{1,17},{17,1},{2,18},{18,2},{3,19},{19,3},{4,20},{20... | collective-permute-start | bytes 49160 | tf_op jit(solution)/shard_map/ppermute | solution.py:17
  184.6 5.4 %collective-permute-start.15 = (f32[2]{0:T(128)S(1)}, f32[2]{0:T(128)S(1)}, u32[]{:S(2)}, u32[]{:S(2)}) collective-permute-start(f32[2]{0:T(128)S(1)} %pad_maximum_fusion.3), channel_id=1, source_target_pairs={{0,1},{1,2},{2,3},{3,0},{4,5},{5,6},{6,7},{7,4},{8,9},{9,10},{10,1... | collective-permute-start | bytes 32 | tf_op jit(solution)/shard_map/ppermute | solution.py:22
  184.6 5.4 %collective-permute-start.14 = (f32[2]{0:T(128)S(1)}, f32[2]{0:T(128)S(1)}, u32[]{:S(2)}, u32[]{:S(2)}) collective-permute-start(f32[2]{0:T(128)S(1)} %pad_maximum_fusion.3), channel_id=1, source_target_pairs={{0,2},{1,3},{2,0},{3,1},{4,6},{5,7},{6,4},{7,5},{8,10},{9,11},{10,... | collective-permute-start | bytes 32 | tf_op jit(solution)/shard_map/ppermute | solution.py:22
  185.3 5.2 %collective-permute-start.13 = (f32[2]{0:T(128)S(1)}, f32[2]{0:T(128)S(1)}, u32[]{:S(2)}, u32[]{:S(2)}) collective-permute-start(f32[2]{0:T(128)S(1)} %pad_maximum_fusion.3), channel_id=1, source_target_pairs={{0,3},{1,0},{2,1},{3,2},{4,7},{5,4},{6,5},{7,6},{8,11},{9,8},{10,9... | collective-permute-start | bytes 32 | tf_op jit(solution)/shard_map/ppermute | solution.py:22
